TPU v7x, 32 devices: a whole 2x2x4 slice. The times are simulated.
32 devices in a mesh: dp: 4 (over y, core), ctx: 2 (over x), tensor: 4 (over z).
Axes of the slice: x: 2, y: 2, z: 4, core: 2. Of those that a mesh axis runs over, the one named last changes fastest.
Arguments:
- layer_input: bfloat16 [4, 512, 8192], P('dp', ('ctx', 'tensor')), may hold values from -6 to 6
- queries: bfloat16 [4, 512, 8192], P('dp', 'ctx', 'tensor'), may hold values from -12 to 12
- forward_output: bfloat16 [4, 512, 8192], P('dp', 'ctx', 'tensor'), may hold values from -6 to 6
- attention_output_gradient: bfloat16 [4, 512, 8192], P('dp', 'ctx', 'tensor'), may hold values from -6 to 6
- key_weight: bfloat16 [8192, 1024], P(None, 'tensor'), may hold values from -3 to 3
- value_projection_weight: bfloat16 [8192, 1024], P(None, 'tensor'), may hold values from -0.0625 to 0.0625
- segment: int32 [4, 512], P('dp'), may hold values from 0 to 4, as said below
- block_table: int32 [4, 4, 4], P('dp'), may hold values from 0 to 1, as said below
- block_owner: int32 [4, 4], P('dp'), may hold values from 0 to 3, each once within a row
Outputs:
- query_grad: bfloat16 [4, 512, 8192], P('dp', 'ctx', 'tensor')
- input_grad: bfloat16 [4, 512, 8192], P('dp', ('ctx', 'tensor'))
- key_weight_grad: bfloat16 [8192, 1024], P(('dp', 'ctx'), 'tensor')
- value_weight_grad: bfloat16 [8192, 1024], P(('dp', 'ctx'), 'tensor')
Inputs may be any that keep to these rules, and one draw needn't show every extreme that they name: Along the logical positions of a group the segment never falls; the prompt (0) comes first and every rollout 1 to 4 is present. block_table[g, b, c] is 1 only where some position of logical block b may read some position of logical block c under the causal and segment rule; block_table[g, b, b] is 1 for every block; other such pairs may be 0. `block_owner`: each group's row holds every logical block once.
All inputs are finite; a program needn't handle non-finite values.
Results may differ from a plain program's by a relative error of at most 0.005.
The roundings to bfloat16 on the way count: a program that leaves them out, or rounds other values in their place, can miss the bound.
Values may be sent and summed in bfloat16 or wider, within the bound.
A program may use at most 128 MiB of HBM per device.

v0:
```python
import math

import jax
import jax.numpy as jnp
from jax import lax
from jax.sharding import PartitionSpec as P

HEAD_SIZE = 128
BLK = 128


def per_device(
    layer_input,
    queries,
    forward_output,
    attention_output_gradient,
    key_weight,
    value_projection_weight,
    segment,
    block_table,
    block_owner,
):
    softmax_scale = 1.0 / math.sqrt(HEAD_SIZE)
    local_rows = queries.shape[1]
    kv_local = key_weight.shape[1] // HEAD_SIZE
    q_local = queries.shape[2] // HEAD_SIZE
    queries_per_group = q_local // kv_local
    kv_width = kv_local * HEAD_SIZE
    gathered = lax.all_gather(layer_input, "tensor", axis=1, tiled=True)[0]
    projected_keys = jnp.dot(gathered, key_weight, preferred_element_type=jnp.float32)
    projected_values = jnp.dot(
        gathered, value_projection_weight, preferred_element_type=jnp.float32
    )
    kv_rows = jnp.concatenate([projected_keys, projected_values], axis=1).astype(jnp.bfloat16)
    owner_row = block_owner[0]
    segments_row = segment[0]
    table_row = block_table[0]
    blocks_here = local_rows // BLK
    ctx_index = lax.axis_index("ctx")
    own_blocks = lax.dynamic_slice_in_dim(owner_row, ctx_index * blocks_here, blocks_here)
    offsets = jnp.arange(BLK, dtype=jnp.int32)
    query_pos = (own_blocks[:, None] * BLK + offsets[None, :]).reshape(-1)
    query_seg = jnp.take(segments_row, query_pos)
    own_table = jnp.take(table_row, own_blocks, axis=0)
    query_heads = queries[0].reshape(local_rows, kv_local, queries_per_group, HEAD_SIZE)
    grad_heads = attention_output_gradient[0].reshape(
        local_rows, kv_local, queries_per_group, HEAD_SIZE
    )
    saved_heads = forward_output[0].reshape(local_rows, kv_local, queries_per_group, HEAD_SIZE)
    correction = jnp.sum(grad_heads.astype(jnp.float32) * saved_heads.astype(jnp.float32), axis=-1)
    correction = correction.transpose(1, 2, 0)

    def allowed_for(leading_row, row_count):
        key_blocks = lax.dynamic_slice_in_dim(owner_row, leading_row // BLK, row_count // BLK)
        key_pos = (key_blocks[:, None] * BLK + offsets[None, :]).reshape(-1)
        key_seg = jnp.take(segments_row, key_pos)
        table_part = jnp.take(own_table, key_blocks, axis=1) == 1
        table_full = jnp.broadcast_to(
            table_part[:, None, :, None], (blocks_here, BLK, row_count // BLK, BLK)
        )
        table_full = table_full.reshape(local_rows, row_count)
        same_tree = (key_seg[None, :] == 0) | (key_seg[None, :] == query_seg[:, None])
        return table_full & (key_pos[None, :] <= query_pos[:, None]) & same_tree

    def block_scores(block_rows, leading_row):
        row_count = block_rows.shape[0]
        block_keys = block_rows[:, :kv_width].reshape(row_count, kv_local, HEAD_SIZE)
        block_values = block_rows[:, kv_width:].reshape(row_count, kv_local, HEAD_SIZE)
        raw_scores = (
            jnp.einsum(
                "qhgd,khd->hgqk", query_heads, block_keys, preferred_element_type=jnp.float32
            )
            * softmax_scale
        )
        allowed = allowed_for(leading_row, row_count)
        return (jnp.where(allowed[None, None], raw_scores, -jnp.inf), block_keys, block_values)

    def stats_block(carried, block_rows, leading_row):
        running_max, running_sum = carried
        scores = block_scores(block_rows, leading_row)[0]
        new_max = jnp.maximum(running_max, jnp.max(scores, axis=-1))
        running_sum = running_sum * jnp.exp(running_max - new_max) + jnp.sum(
            jnp.exp(scores - new_max[..., None]), axis=-1
        )
        return (new_max, running_sum)

    def grads_block(carried, block_rows, leading_row, log_norm):
        query_sum, keyval_sum = carried
        row_count = block_rows.shape[0]
        scores, block_keys, block_values = block_scores(block_rows, leading_row)
        probabilities = jnp.exp(scores - log_norm[..., None])
        probs_low = probabilities.astype(jnp.bfloat16)
        value_gradient_rows = jnp.einsum(
            "hgqk,qhgd->khd", probs_low, grad_heads, preferred_element_type=jnp.float32
        )
        prob_grads = jnp.einsum(
            "qhgd,khd->hgqk", grad_heads, block_values, preferred_element_type=jnp.float32
        )
        score_low = (probabilities * (prob_grads - correction[..., None])).astype(jnp.bfloat16)
        query_sum = query_sum + jnp.einsum(
            "hgqk,khd->qhgd", score_low, block_keys, preferred_element_type=jnp.float32
        )
        key_gradient_rows = (
            jnp.einsum("hgqk,qhgd->khd", score_low, query_heads, preferred_element_type=jnp.float32)
            * softmax_scale
        )
        update = jnp.concatenate(
            [
                key_gradient_rows.reshape(row_count, kv_width),
                value_gradient_rows.reshape(row_count, kv_width),
            ],
            axis=1,
        )
        keyval_sum = lax.dynamic_update_slice_in_dim(keyval_sum, update, leading_row, 0)
        return (query_sum, keyval_sum)

    def over_blocks(block_step, carried, shard_part):
        row_count = shard_part.shape[0]
        block_size = math.gcd(row_count, max(512, local_rows))
        block_count = row_count // block_size
        pieces = shard_part.reshape(block_count, block_size, shard_part.shape[1])
        starts = block_size * jnp.arange(block_count, dtype=jnp.int32)

        def one_block(state_in, scan_item):
            block_rows, block_start = scan_item
            result = block_step(state_in, block_rows, block_start)
            return (result, None)

        carried, _ = lax.scan(one_block, carried, (pieces, starts))
        return carried

    stats_init = (
        jnp.full((kv_local, queries_per_group, local_rows), -1e30, jnp.float32),
        jnp.zeros((kv_local, queries_per_group, local_rows), jnp.float32),
    )
    seq_rows = local_rows * lax.axis_size("ctx")
    grads_init = (
        jnp.zeros((local_rows, kv_local, queries_per_group, HEAD_SIZE), jnp.float32),
        jnp.zeros((seq_rows, 2 * kv_width), jnp.float32),
    )
    running_max, running_sum = over_blocks(
        stats_block, stats_init, lax.all_gather(kv_rows, "ctx", axis=0, tiled=True)
    )
    log_norm = running_max + jnp.log(running_sum)

    def grads_fold(carried, shard_part):
        return over_blocks(
            lambda state, rows_in, start_in: grads_block(state, rows_in, start_in, log_norm),
            carried,
            shard_part,
        )

    query_sum, keyval_sum = grads_fold(
        grads_init, lax.all_gather(kv_rows, "ctx", axis=0, tiled=True)
    )
    own_grads = lax.psum_scatter(keyval_sum, "ctx", scatter_dimension=0, tiled=True).astype(
        jnp.bfloat16
    )
    query_grad = (
        (query_sum * softmax_scale).astype(jnp.bfloat16).reshape(1, local_rows, q_local * HEAD_SIZE)
    )
    term = lax.dot_general(
        own_grads[:, :kv_width],
        key_weight,
        (((1,), (1,)), ((), ())),
        preferred_element_type=jnp.float32,
    )
    input_grad = lax.psum_scatter(
        term
        + lax.dot_general(
            own_grads[:, kv_width:],
            value_projection_weight,
            (((1,), (1,)), ((), ())),
            preferred_element_type=jnp.float32,
        ),
        "tensor",
        scatter_dimension=0,
        tiled=True,
    )
    input_grad = input_grad.astype(jnp.bfloat16)[None]
    weight_sum = lax.psum_scatter(
        lax.dot_general(
            gathered, own_grads, (((0,), (0,)), ((), ())), preferred_element_type=jnp.float32
        ),
        ("dp", "ctx"),
        scatter_dimension=0,
        tiled=True,
    )
    key_weight_grad = weight_sum[:, :kv_width].astype(jnp.bfloat16)
    value_weight_grad = weight_sum[:, kv_width:].astype(jnp.bfloat16)
    return (query_grad, input_grad, key_weight_grad, value_weight_grad)


def solution(mesh):
    in_specs = (
        P("dp", ("ctx", "tensor"), None),
        P("dp", "ctx", "tensor"),
        P("dp", "ctx", "tensor"),
        P("dp", "ctx", "tensor"),
        P(None, "tensor"),
        P(None, "tensor"),
        P("dp", None),
        P("dp", None, None),
        P("dp", None),
    )
    out_specs = (
        P("dp", "ctx", "tensor"),
        P("dp", ("ctx", "tensor"), None),
        P(("dp", "ctx"), "tensor"),
        P(("dp", "ctx"), "tensor"),
    )
    return jax.shard_map(
        per_device, mesh=mesh, in_specs=in_specs, out_specs=out_specs, check_vma=False
    )
```

profile of v0, /device:TPU:14, one launch (start us, length us, event | category | flops | bytes accessed | tf_op | source)
XLA Modules:
  0.0 424.2 jit_solution(8074572103710751653)
XLA Ops:
  7.3 0.7 all-gather.2.cloned.1.call-update
  8.0 0.7 bitcast_multiply_fusion.1
  8.7 3.5 gather_fusion.3
  12.3 0.8 bitcast_multiply_fusion
  13.2 1.9 gather_fusion.1
  18.2 1.6 copy.71
  19.8 1.6 copy.53
  22.0 0.9 multiply_reduce_fusion
  23.1 66.1 %all-gather.2.cloned.1.call-done = bf16[1,256,8192]{2,1,0:T(8,128)(2,1)} async-done(((bf16[1,64,8192]{2,1,0:T(8,128)(2,1)}), bf16[1,256,8192]{2,1,0:T(8,128)(2,1)}) %all-gather.2.cloned.1.call-update) | async-done | bytes 4194320 | tf_op jit(solution)/shard_map/all_gather | solution.py:29
  89.1 5.3 %fusion.16 = bf16[256,256]{0,1:T(8,128)(2,1)S(1)} fusion(bf16[8192,256]{1,0:T(8,128)(2,1)} %param.18, bf16[1,256,8192]{2,1,0:T(8,128)(2,1)} %all-gather.2.cloned.1.call-done), kind=kOutput, calls=%fused_computation.27 | convolution fusion | flops 1073807360 | bytes 8519680 | tf_op jit(solution)/shard_map/dot_general | solution.py:31
  95.0 1.9 fusion.13
  96.9 9.0 %all_gather.8 = bf16[512,512]{0,1:T(8,128)(2,1)S(1)} all-gather(bf16[256,512]{0,1:T(8,128)(2,1)S(1)} %pad_maximum_fusion.1), channel_id=1, replica_groups=mesh['dp'=4,'ctx'=2,'tensor'=4] {'ctx'}, dimensions={0}, use_global_device_ids=true | all-gather | bytes 786432 | tf_op jit(solution)/shard_map/all_gather | solution.py:154
  106.0 1.4 fusion.3
  107.4 1.7 exponential_reduce_fusion
  109.1 2.3 fusion.9
  111.4 2.9 fusion.1
  114.3 2.0 copy-done.5
  116.3 1.5 fusion.12
  117.7 1.0 pad_maximum_fusion
  118.9 20.5 %reduce-scatter.4.cloned.1.call-done = f32[256,512]{0,1:T(8,128)} async-done(((f32[512,512]{0,1:T(8,128)}), f32[256,512]{0,1:T(8,128)}) %reduce-scatter.4.cloned.1.call-update) | async-done | bytes 524304 | tf_op jit(solution)/shard_map/reduce_scatter | solution.py:156
  139.4 1.1 convert_element_type.47
  140.4 3.6 fusion.21
  144.1 4.5 %convolution_add_fusion = f32[256,8192]{1,0:T(8,128)} fusion(f32[256,8192]{1,0:T(8,128)S(1)} %fusion.21, bf16[8192,256]{1,0:T(8,128)(2,1)S(1)} %copy-done.4, bf16[256,512]{0,1:T(8,128)(2,1)S(1)} %convert_element_type.47), kind=kOutput, calls=%fused_computation.5 | convolution fusion | flops 1075838976 | bytes 21102592 | tf_op jit(solution)/shard_map/dot_general | solution.py:170
  148.9 10.9 %convolution_bitcast_fusion = f32[8192,512]{0,1:T(8,128)} fusion(bf16[256,512]{0,1:T(8,128)(2,1)S(1)} %convert_element_type.47, bf16[1,256,8192]{2,1,0:T(8,128)(2,1)} %all-gather.2.cloned.1.call-done), kind=kOutput, calls=%fused_computation.4 | convolution fusion | flops 2147483648 | bytes 21233664 | tf_op jit(solution)/shard_map/dot_general | solution.py:182
  159.9 2.9 multiply_convert_fusion
  162.8 1.4 copy.54
  164.2 129.7 %reduce-scatter.6.cloned.1.call-done = f32[64,8192]{1,0:T(8,128)} async-done(((f32[256,8192]{1,0:T(8,128)}), f32[64,8192]{1,0:T(8,128)}) %reduce-scatter.6.cloned.1.call-update) | async-done | bytes 2097168 | tf_op jit(solution)/shard_map/reduce_scatter | solution.py:168
  293.9 2.7 convert_bitcast_fusion.1
  296.6 117.3 %reduce-scatter.8.cloned.1.call-done = f32[1024,512]{0,1:T(8,128)} async-done(((f32[8192,512]{0,1:T(8,128)}), f32[1024,512]{0,1:T(8,128)}) %reduce-scatter.8.cloned.1.call-update) | async-done | bytes 2097168 | tf_op jit(solution)/shard_map/reduce_scatter | solution.py:181
  413.9 1.7 convert.13
  415.7 1.0 copy.56
  416.7 1.0 copy.55
  (59 shorter events, 5.1 us)
Async XLA Ops:
  7.2 1.6 copy-start
  7.2 8.0 %copy-start.10 = (s32[1,4]{1,0:T(1,128)S(1)}, s32[1,4]{1,0:T(1,128)}, u32[]{:S(2)}) copy-start(s32[1,4]{1,0:T(1,128)} %param.21) | copy-start | bytes 52
  7.2 8.1 %copy-start.9 = (s32[1,4,4]{2,1,0:T(4,128)S(1)}, s32[1,4,4]{2,1,0:T(4,128)}, u32[]{:S(2)}) copy-start(s32[1,4,4]{2,1,0:T(4,128)} %param.20) | copy-start | bytes 196
  7.2 10.5 %copy-start.7 = (bf16[1,256,2048]{2,1,0:T(8,128)(2,1)S(1)}, bf16[1,256,2048]{2,1,0:T(8,128)(2,1)}, u32[]{:S(2)}) copy-start(bf16[1,256,2048]{2,1,0:T(8,128)(2,1)} %param.14) | copy-start | bytes 3145732
  7.2 81.9 %all-gather.2.cloned.1.call-start = ((), (), s32[]{:S(2)}) async-start(), calls=%async_computation.3 | async-start | bytes 5242880 | tf_op jit(solution)/shard_map/all_gather | solution.py:29
  7.9 131.4 %reduce-scatter.4.cloned.1.call-start = ((), (), s32[]{:S(2)}) async-start(), calls=%async_computation.4 | async-start | bytes 1572864 | tf_op jit(solution)/shard_map/reduce_scatter | solution.py:156
  12.3 9.1 %copy-start.6 = (bf16[1,256,2048]{2,1,0:T(8,128)(2,1)S(1)}, bf16[1,256,2048]{2,1,0:T(8,128)(2,1)}, u32[]{:S(2)}) copy-start(bf16[1,256,2048]{2,1,0:T(8,128)(2,1)} %param.15) | copy-start | bytes 3145732
  89.1 5.3 %copy-start.2 = (bf16[1,256,8192]{2,1,0:T(8,128)(2,1)S(1)}, bf16[1,256,8192]{2,1,0:T(8,128)(2,1)}, u32[]{:S(2)}) copy-start(bf16[1,256,8192]{2,1,0:T(8,128)(2,1)} %all-gather.2.cloned.1.call-done) | copy-start | bytes 12582916
  89.1 5.9 %copy-start.3 = (bf16[8192,256]{1,0:T(8,128)(2,1)S(1)}, bf16[8192,256]{1,0:T(8,128)(2,1)}, u32[]{:S(2)}) copy-start(bf16[8192,256]{1,0:T(8,128)(2,1)} %param.17) | copy-start | bytes 12582916
  107.4 1.8 copy-start.8
  114.3 2.0 copy-start.5
  118.8 175.1 %reduce-scatter.6.cloned.1.call-start = ((), (), s32[]{:S(2)}) async-start(), calls=%async_computation.5 | async-start | bytes 10485760 | tf_op jit(solution)/shard_map/reduce_scatter | solution.py:168
  140.4 3.7 copy-start.4
  148.7 265.2 %reduce-scatter.8.cloned.1.call-start = ((), (), s32[]{:S(2)}) async-start(), calls=%async_computation.6 | async-start | bytes 18874368 | tf_op jit(solution)/shard_map/reduce_scatter | solution.py:181
  293.9 123.8 %copy-start.1 = (s32[1,512]{1,0:T(1,128)S(1)}, s32[1,512]{1,0:T(1,128)}, u32[]{:S(2)}) copy-start(s32[1,512]{1,0:T(1,128)} %param.19) | copy-start | bytes 6148
Sparse Core Ops, SparseCore 0:
  9.6 79.4 all-gather.1
  118.9 20.3 reduce-scatter.3
  148.8 145.0 reduce-scatter.5
  297.8 116.0 reduce-scatter.7
where the time goes:
time: 427 us; the launch traced here: 424 us
  waiting for transfers between devices  334 us (78%)
  matrix products  37.2 us (9%)
  local copies, waits for them, and re-layouts  17.5 us (4%)
  between operations  14.1 us (3%)
  other arithmetic  11.9 us (3%)
  blocking collectives  8.98 us (2%)
    reduce_scatter x1, waiting for transfers between devices, per_device(): lax.psum_scatter(term + lax.dot_general(own_grads[:, kv_width:], value_pr...  130 us
    reduce_scatter x1, waiting for transfers between devices, per_device(): lax.psum_scatter(lax.dot_general(gathered, own_grads, (((0,), (0,)), ((),...  117 us
    all_gather x1, waiting for transfers between devices, per_device(): gathered = lax.all_gather(layer_input, 'tensor', axis=1, tiled=True)[0]  66.1 us
    reduce_scatter x1, waiting for transfers between devices, per_device(): lax.psum_scatter(keyval_sum, 'ctx', scatter_dimension=0, tiled=True)  20.5 us
    dot_general x1, matrix products, per_device(): lax.dot_general(gathered, own_grads, (((0,), (0,)), ((), ())), preferred_...  10.9 us
    all_gather x1, blocking collectives, per_device(): lax.all_gather(kv_rows, 'ctx', axis=0, tiled=True)  8.98 us
  transfers between devices with their start and end apart: 4, of which 4 were waited for; matrix products, arithmetic and copies ran while one was open for 8% of the time, Pallas kernels for 0%

commit v1 on v0

--- a/solution.py
+++ b/solution.py
@@ -27,6 +27,20 @@
     queries_per_group = q_local // kv_local
     kv_width = kv_local * HEAD_SIZE
     gathered = lax.all_gather(layer_input, "tensor", axis=1, tiled=True)[0]
+    planes = lax.axis_size("tensor")
+    plane_size = lax.axis_size("dp") * lax.axis_size("ctx")
+    plane_index = lax.axis_index("dp") * lax.axis_size("ctx") + lax.axis_index("ctx")
+    model_width = key_weight.shape[0]
+    piece_rows = model_width // (planes * plane_size)
+
+    def piece(weight):
+        split = weight.reshape(planes, plane_size, piece_rows, kv_width)
+        return lax.dynamic_index_in_dim(split, plane_index, 1, keepdims=False)
+
+    pieces = jnp.concatenate([piece(key_weight), piece(value_projection_weight)], axis=2)
+    pieces = lax.all_to_all(pieces, "tensor", split_axis=0, concat_axis=0, tiled=True)
+    wide_weight = lax.all_gather(pieces, ("dp", "ctx"), axis=1, tiled=True)
+    plane_input = lax.all_to_all(gathered, ("dp", "ctx"), split_axis=1, concat_axis=0, tiled=True)
     projected_keys = jnp.dot(gathered, key_weight, preferred_element_type=jnp.float32)
     projected_values = jnp.dot(
         gathered, value_projection_weight, preferred_element_type=jnp.float32
@@ -159,32 +173,14 @@
     query_grad = (
         (query_sum * softmax_scale).astype(jnp.bfloat16).reshape(1, local_rows, q_local * HEAD_SIZE)
     )
-    term = lax.dot_general(
-        own_grads[:, :kv_width],
-        key_weight,
-        (((1,), (1,)), ((), ())),
-        preferred_element_type=jnp.float32,
-    )
-    input_grad = lax.psum_scatter(
-        term
-        + lax.dot_general(
-            own_grads[:, kv_width:],
-            value_projection_weight,
-            (((1,), (1,)), ((), ())),
-            preferred_element_type=jnp.float32,
-        ),
-        "tensor",
-        scatter_dimension=0,
-        tiled=True,
-    )
-    input_grad = input_grad.astype(jnp.bfloat16)[None]
-    weight_sum = lax.psum_scatter(
-        lax.dot_general(
-            gathered, own_grads, (((0,), (0,)), ((), ())), preferred_element_type=jnp.float32
-        ),
-        ("dp", "ctx"),
-        scatter_dimension=0,
-        tiled=True,
+    kv_all = lax.all_gather(own_grads, "tensor", axis=0)
+    kv_plane = lax.all_gather(own_grads, ("dp", "ctx"), axis=0, tiled=True)
+    width_part = lax.dot_general(
+        kv_all, wide_weight, (((0, 2), (0, 2)), ((), ())), preferred_element_type=jnp.float32
+    ).astype(jnp.bfloat16)
+    input_grad = lax.all_to_all(width_part, "tensor", split_axis=0, concat_axis=1, tiled=True)[None]
+    weight_sum = lax.dot_general(
+        plane_input, kv_plane, (((0,), (0,)), ((), ())), preferred_element_type=jnp.float32
     )
     key_weight_grad = weight_sum[:, :kv_width].astype(jnp.bfloat16)
     value_weight_grad = weight_sum[:, kv_width:].astype(jnp.bfloat16)

time: 427 us -> 302 us (0.71)
  waiting for transfers between devices: 334 us -> 180 us
  local copies, waits for them, and re-layouts: 17.5 us -> 37.1 us
  starting transfers between devices: 0.38 us -> 16.9 us
  matrix products: 37.2 us -> 30 us
    reduce_scatter x2 -> x0, waiting for transfers between devices: 247 us -> none  [the longest x1 130 us: per_device(): lax.psum_scatter(term + lax.dot_general(own_grads[:, kv_width:], value_pr...]
    all_gather x0 -> x3, waiting for transfers between devices: none -> 95.5 us  [the longest x1 78.9 us: per_device(): wide_weight = lax.all_gather(pieces, ('dp', 'ctx'), axis=1, tiled=True)]
    all_to_all x0 -> x3, starting transfers between devices: none -> 16.8 us  [the longest x1 6.53 us: per_device(): lax.all_to_all(pieces, 'tensor', split_axis=0, concat_axis=0, tiled=True)]
    reduce_scatter x1, waiting for transfers between devices: 20.5 us -> 11.7 us  [per_device(): lax.psum_scatter(keyval_sum, 'ctx', scatter_dimension=0, tiled=True)]
    all_to_all x0 -> x3, waiting for transfers between devices: none -> 8.2 us  [the longest x1 8.19 us: per_device(): lax.all_to_all(pieces, 'tensor', split_axis=0, concat_axis=0, tiled=True)]
    all_gather x0 -> x2, local copies, waits for them, and re-layouts: none -> 7.86 us  [the longest x1 6.36 us: per_device(): gathered = lax.all_gather(layer_input, 'tensor', axis=1, tiled=True)[0]]
    all_to_all x0 -> x2, local copies, waits for them, and re-layouts: none -> 7.25 us  [the longest x1 6.44 us: per_device(): lax.all_to_all(gathered, ('dp', 'ctx'), split_axis=1, concat_axis=0, tile...]
    dot_general x3 -> x2, matrix products: 19.1 us -> 11.9 us  [the longest x1 6.71 us: per_device(): lax.dot_general(kv_all, wide_weight, (((0, 2), (0, 2)), ((), ())), prefer...]
  transfers between devices with their start and end apart: 4 -> 8, of which waited for: 4 -> 6; matrix products, arithmetic and copies ran while one was open for 8% -> 18% of each run, Pallas kernels for 0% -> 0%
where the time goes in v1:
time: 302 us; the launch traced here: 298 us
  waiting for transfers between devices  180 us (60%)
  local copies, waits for them, and re-layouts  37.1 us (12%)
  matrix products  30 us (10%)
  starting transfers between devices  16.9 us (6%)
  between operations  14 us (5%)
  other arithmetic  11.1 us (4%)
  blocking collectives  8.86 us (3%)
    all_gather x1, waiting for transfers between devices, per_device(): wide_weight = lax.all_gather(pieces, ('dp', 'ctx'), axis=1, tiled=True)  78.9 us
    all_gather x1, waiting for transfers between devices, per_device(): gathered = lax.all_gather(layer_input, 'tensor', axis=1, tiled=True)[0]  63.6 us
    reduce_scatter x1, waiting for transfers between devices, per_device(): lax.psum_scatter(keyval_sum, 'ctx', scatter_dimension=0, tiled=True)  11.7 us
    unnamed x23, local copies, waits for them, and re-layouts  8.89 us
    all_gather x1, blocking collectives, per_device(): lax.all_gather(kv_rows, 'ctx', axis=0, tiled=True)  8.86 us
    all_gather x1, waiting for transfers between devices, per_device(): kv_all = lax.all_gather(own_grads, 'tensor', axis=0)  8.51 us
    all_to_all x1, waiting for transfers between devices, per_device(): lax.all_to_all(pieces, 'tensor', split_axis=0, concat_axis=0, tiled=True)  8.19 us
    all_gather x1, waiting for transfers between devices, per_device(): kv_plane = lax.all_gather(own_grads, ('dp', 'ctx'), axis=0, tiled=True)  8.05 us
  transfers between devices with their start and end apart: 8, of which 6 were waited for; matrix products, arithmetic and copies ran while one was open for 18% of the time, Pallas kernels for 0%

profile of v1, /device:TPU:14, one launch (start us, length us, event | category | flops | bytes accessed | tf_op | source)
XLA Modules:
  0.0 298.2 jit_solution(7361246667366215008)
XLA Ops:
  13.8 1.9 gather_fusion.1
  15.8 3.5 %gather_fusion.3 = s32[512]{0:T(512)S(1)} fusion(s32[512]{0:T(512)S(1)} %bitcast.138, s32[1024]{0:T(1024)S(1)} %pad_clamp_fusion.1), kind=kCustom, calls=%fused_computation.1.clone | custom fusion | bytes 6144 | tf_op jit(solution)/shard_map/while/body/eval_jaxpr/jit(_take)/gather | solution.py:70
  20.8 1.5 copy.108
  22.3 1.6 copy.82
  25.5 63.6 %all-gather.6.cloned.1.call-done = bf16[1,256,8192]{2,1,0:T(8,128)(2,1)} async-done(((bf16[1,64,8192]{2,1,0:T(8,128)(2,1)}), bf16[1,256,8192]{2,1,0:T(8,128)(2,1)}) %all-gather.6.cloned.1.call-update) | async-done | bytes 4194320 | tf_op jit(solution)/shard_map/all_gather | solution.py:29
  89.1 5.3 %fusion.14 = bf16[256,256]{0,1:T(8,128)(2,1)S(1)} fusion(bf16[8192,256]{1,0:T(8,128)(2,1)} %param.17, bf16[1,256,8192]{2,1,0:T(8,128)(2,1)} %all-gather.6.cloned.1.call-done), kind=kOutput, calls=%fused_computation.27 | convolution fusion | flops 1073807360 | bytes 8519680 | tf_op jit(solution)/shard_map/dot_general | solution.py:44
  95.0 1.9 fusion.17
  96.9 8.9 %all_gather.20 = bf16[512,512]{0,1:T(8,128)(2,1)S(1)} all-gather(bf16[256,512]{0,1:T(8,128)(2,1)S(1)} %pad_maximum_fusion.2), channel_id=1, replica_groups=mesh['dp'=4,'ctx'=2,'tensor'=4] {'ctx'}, dimensions={0}, use_global_device_ids=true | all-gather | bytes 786432 | tf_op jit(solution)/shard_map/all_gather | solution.py:168
  105.8 1.4 fusion.3
  107.2 1.7 exponential_reduce_fusion
  109.0 2.3 fusion.8
  111.3 2.9 fusion.1
  114.2 2.0 copy-done.3
  116.1 1.5 fusion.13
  118.7 1.3 dynamic-slice_bitcast_fusion
  121.0 6.5 %all-to-all-start = ((bf16[4,256,512]{2,1,0:T(8,128)(2,1)}), bf16[4,256,512]{2,1,0:T(8,128)(2,1)S(1)}, u32[]{:S(2)}, u32[]{:S(2)}) async-start(bf16[4,256,512]{2,1,0:T(8,128)(2,1)} %pad_maximum_fusion.1), calls=%async_computation.1 | async-start | bytes 2097152 | tf_op jit(solution)/shard_map/all_to_all | solution.py:41
  127.6 11.7 %reduce-scatter.2.cloned.1.call-done = f32[256,512]{0,1:T(8,128)} async-done(((f32[512,512]{0,1:T(8,128)}), f32[256,512]{0,1:T(8,128)}) %reduce-scatter.2.cloned.1.call-update) | async-done | bytes 524304 | tf_op jit(solution)/shard_map/reduce_scatter | solution.py:170
  139.3 1.8 convert_element_type.47
  141.1 8.2 %all-to-all-done = bf16[4,256,512]{2,1,0:T(8,128)(2,1)S(1)} async-done(((bf16[4,256,512]{2,1,0:T(8,128)(2,1)}), bf16[4,256,512]{2,1,0:T(8,128)(2,1)S(1)}, u32[]{:S(2)}, u32[]{:S(2)}) %all-to-all-start) | async-done | bytes 1048608 | tf_op jit(solution)/shard_map/all_to_all | solution.py:41
  150.3 6.4 %copy.87 = bf16[1,256,8192]{1,2,0:T(8,128)(2,1)} copy(bf16[1,256,8192]{2,1,0:T(8,128)(2,1)} %all-gather.6.cloned.1.call-done) | data formatting | bytes 8388608 | tf_op jit(solution)/shard_map/all_gather | solution.py:29
  156.7 5.1 %all-to-all-start.2 = ((bf16[256,8,1024]{0,2,1:T(8,128)(2,1)}), bf16[256,8,1024]{0,2,1:T(8,128)(2,1)}, u32[]{:S(2)}, u32[]{:S(2)}) async-start(bf16[256,8,1024]{0,2,1:T(8,128)(2,1)} %bitcast.140), calls=%async_computation.3 | async-start | bytes 8388608 | tf_op jit(solution)/shard_map/all_to_all | solution.py:43
  162.4 8.5 %all-gather.12.cloned.1.call-done = bf16[1024,512]{0,1:T(8,128)(2,1)} async-done(((bf16[256,512]{0,1:T(8,128)(2,1)}), bf16[1024,512]{0,1:T(8,128)(2,1)}) %all-gather.12.cloned.1.call-update) | async-done | bytes 1048592 | tf_op jit(solution)/shard_map/all_gather | solution.py:176
  170.9 1.5 copy.83
  172.4 78.9 %all-gather.8.cloned.1.call-done = bf16[4,2048,512]{2,1,0:T(8,128)(2,1)} async-done(((bf16[4,256,512]{2,1,0:T(8,128)(2,1)}), bf16[4,2048,512]{2,1,0:T(8,128)(2,1)}) %all-gather.8.cloned.1.call-update) | async-done | bytes 8388624 | tf_op jit(solution)/shard_map/all_gather | solution.py:42
  251.3 6.7 %fusion.11 = bf16[256,2048]{1,0:T(8,128)(2,1)} fusion(bf16[4,256,512]{2,1,0:T(8,128)(2,1)S(1)} %bitcast.155, bf16[4,2048,512]{2,1,0:T(8,128)(2,1)} %all-gather.8.cloned.1.call-done), kind=kOutput, calls=%fused_computation.19 | convolution fusion | flops 2148007936 | bytes 10485760 | tf_op jit(solution)/shard_map/dot_general | solution.py:178
  258.1 5.1 %all-to-all-start.1 = ((bf16[4,64,2048]{2,1,0:T(8,128)(2,1)}), bf16[4,64,2048]{2,1,0:T(8,128)(2,1)S(1)}, u32[]{:S(2)}, u32[]{:S(2)}) async-start(bf16[4,64,2048]{2,1,0:T(8,128)(2,1)} %bitcast.37), calls=%async_computation.2 | async-start | bytes 2097152 | tf_op jit(solution)/shard_map/all_to_all | solution.py:181
  263.2 2.9 multiply_convert_fusion
  266.1 1.4 copy.89
  267.5 6.4 %copy.88 = bf16[8,256,1024]{2,1,0:T(8,128)(2,1)} copy(bf16[8,256,1024]{1,2,0:T(8,128)(2,1)} %bitcast.40) | data formatting | bytes 8388608 | tf_op jit(solution)/shard_map/all_to_all | solution.py:43
  274.0 8.0 %all-gather.10.cloned.1.call-done = bf16[2048,512]{0,1:T(8,128)(2,1)} async-done(((bf16[256,512]{0,1:T(8,128)(2,1)}), bf16[2048,512]{0,1:T(8,128)(2,1)}) %all-gather.10.cloned.1.call-update) | async-done | bytes 2097168 | tf_op jit(solution)/shard_map/all_gather | solution.py:177
  282.0 5.2 %fusion.12 = bf16[1024,512]{0,1:T(8,128)(2,1)S(1)} fusion(bf16[2048,512]{0,1:T(8,128)(2,1)} %all-gather.10.cloned.1.call-done, bf16[2048,1024]{1,0:T(8,128)(2,1)} %bitcast.148), kind=kOutput, calls=%fused_computation.24 | convolution fusion | flops 2148007936 | bytes 7340032 | tf_op jit(solution)/shard_map/dot_general | solution.py:182
  290.1 1.6 broadcast_in_dim.114
  (68 shorter events, 16.9 us)
Async XLA Ops:
  7.2 6.6 %copy-start = (s32[1,512]{1,0:T(1,128)S(1)}, s32[1,512]{1,0:T(1,128)}, u32[]{:S(2)}) copy-start(s32[1,512]{1,0:T(1,128)} %param.19) | copy-start | bytes 6148
  7.2 13.0 %copy-start.7 = (bf16[1,256,2048]{2,1,0:T(8,128)(2,1)S(1)}, bf16[1,256,2048]{2,1,0:T(8,128)(2,1)}, u32[]{:S(2)}) copy-start(bf16[1,256,2048]{2,1,0:T(8,128)(2,1)} %param.14) | copy-start | bytes 3145732
  7.2 81.9 %all-gather.6.cloned.1.call-start = ((), (), s32[]{:S(2)}) async-start(), calls=%async_computation.4 | async-start | bytes 5242880 | tf_op jit(solution)/shard_map/all_gather | solution.py:29
  7.9 131.4 %reduce-scatter.2.cloned.1.call-start = ((), (), s32[]{:S(2)}) async-start(), calls=%async_computation.5 | async-start | bytes 1572864 | tf_op jit(solution)/shard_map/reduce_scatter | solution.py:170
  15.8 8.1 %copy-start.6 = (bf16[1,256,2048]{2,1,0:T(8,128)(2,1)S(1)}, bf16[1,256,2048]{2,1,0:T(8,128)(2,1)}, u32[]{:S(2)}) copy-start(bf16[1,256,2048]{2,1,0:T(8,128)(2,1)} %param.15) | copy-start | bytes 3145732
  89.1 5.3 %copy-start.2 = (bf16[1,256,8192]{2,1,0:T(8,128)(2,1)S(1)}, bf16[1,256,8192]{2,1,0:T(8,128)(2,1)}, u32[]{:S(2)}) copy-start(bf16[1,256,8192]{2,1,0:T(8,128)(2,1)} %all-gather.6.cloned.1.call-done) | copy-start | bytes 12582916
  89.1 5.9 %copy-start.4 = (bf16[8192,256]{1,0:T(8,128)(2,1)S(1)}, bf16[8192,256]{1,0:T(8,128)(2,1)}, u32[]{:S(2)}) copy-start(bf16[8192,256]{1,0:T(8,128)(2,1)} %param.18) | copy-start | bytes 12582916
  107.2 1.8 copy-start.8
  114.1 2.0 copy-start.3
  121.0 28.3 %all-to-all-start = ((bf16[4,256,512]{2,1,0:T(8,128)(2,1)}), bf16[4,256,512]{2,1,0:T(8,128)(2,1)S(1)}, u32[]{:S(2)}, u32[]{:S(2)}) async-start(bf16[4,256,512]{2,1,0:T(8,128)(2,1)} %pad_maximum_fusion.1), calls=%async_computation.1 | async-start | bytes 2097152 | tf_op jit(solution)/shard_map/all_to_all | solution.py:41
  127.6 43.3 %all-gather.12.cloned.1.call-start = ((), (), s32[]{:S(2)}) async-start(), calls=%async_computation.8 | async-start | bytes 1310720 | tf_op jit(solution)/shard_map/all_gather | solution.py:176
  141.1 110.3 %all-gather.8.cloned.1.call-start = ((), (), s32[]{:S(2)}) async-start(), calls=%async_computation.6 | async-start | bytes 9437184 | tf_op jit(solution)/shard_map/all_gather | solution.py:42
  149.3 1.0 copy-start.5
  156.7 101.4 %all-to-all-start.2 = ((bf16[256,8,1024]{0,2,1:T(8,128)(2,1)}), bf16[256,8,1024]{0,2,1:T(8,128)(2,1)}, u32[]{:S(2)}, u32[]{:S(2)}) async-start(bf16[256,8,1024]{0,2,1:T(8,128)(2,1)} %bitcast.140), calls=%async_computation.3 | async-start | bytes 8388608 | tf_op jit(solution)/shard_map/all_to_all | solution.py:43
  161.8 120.2 %all-gather.10.cloned.1.call-start = ((), (), s32[]{:S(2)}) async-start(), calls=%async_computation.7 | async-start | bytes 2359296 | tf_op jit(solution)/shard_map/all_gather | solution.py:177
  258.1 31.2 %all-to-all-start.1 = ((bf16[4,64,2048]{2,1,0:T(8,128)(2,1)}), bf16[4,64,2048]{2,1,0:T(8,128)(2,1)S(1)}, u32[]{:S(2)}, u32[]{:S(2)}) async-start(bf16[4,64,2048]{2,1,0:T(8,128)(2,1)} %bitcast.37), calls=%async_computation.2 | async-start | bytes 2097152 | tf_op jit(solution)/shard_map/all_to_all | solution.py:181
  282.0 9.7 %copy-start.1 = (s32[1,512]{1,0:T(1,128)S(1)}, s32[1,512]{1,0:T(1,128)}, u32[]{:S(2)}) copy-start(s32[1,512]{1,0:T(1,128)} %param.19) | copy-start | bytes 6148
Sparse Core Ops, SparseCore 0:
  9.6 79.4 all-gather.5
  118.8 20.4 reduce-scatter.1
  141.5 29.3 all-gather.11
  173.4 77.9 all-gather.7
  253.8 28.1 all-gather.9

commit v2 on v1

--- a/solution.py
+++ b/solution.py
@@ -1,12 +1,214 @@
+import functools
 import math
 
 import jax
 import jax.numpy as jnp
 from jax import lax
+from jax.experimental import pallas as pl
+from jax.experimental.pallas import tpu as pltpu
 from jax.sharding import PartitionSpec as P
 
 HEAD_SIZE = 128
 BLK = 128
+
+MESH = pl.DeviceIdType.MESH
+
+
+def exchange_kernel(
+    nt, nd, nc, x_ref, kw_ref, vw_ref, g_ref, xc_ref, wide_ref,
+    x_send, x_recv, w_send, w_recv, p_send, p_recv, f_send, f_recv, s_send, s_recv, local_sem,
+):
+    t = lax.axis_index("tensor")
+    d = lax.axis_index("dp")
+    c = lax.axis_index("ctx")
+    plane = nd * nc
+    half = plane // 2
+    p = d * nc + c
+    h = (d // 2) * nc + c
+    core = d % 2
+    rows, width = x_ref.shape
+    kv = kw_ref.shape[1]
+    chunk = width // nt
+    piece = chunk // plane
+    slice_width = width // plane
+
+    barrier = pltpu.get_barrier_semaphore()
+    for r in range(1, nt):
+        pl.semaphore_signal(
+            barrier, inc=1, device_id={"tensor": (t + r) % nt}, device_id_type=MESH
+        )
+    for r in range(1, plane):
+        q = (p + r) % plane
+        pl.semaphore_signal(
+            barrier, inc=1, device_id={"dp": q // nc, "ctx": q % nc}, device_id_type=MESH
+        )
+    pl.semaphore_wait(barrier, nt - 1 + plane - 1)
+
+    def x_rows(b):
+        return g_ref.at[pl.ds(pl.multiple_of(b * rows, rows), rows), :]
+
+    def x_copy(way, s, source, b, target):
+        return pltpu.make_async_remote_copy(
+            src_ref=source, dst_ref=x_rows(b), send_sem=x_send.at[way, s - 1],
+            recv_sem=x_recv.at[way, s - 1], device_id={"tensor": target}, device_id_type=MESH,
+        )
+
+    def sends(s):
+        for way in (0, 1):
+            step = 1 if way == 0 else -1
+            b = t - step * (s - 1)
+            target = t + step
+            ok = (target >= 0) & (target < nt) & (b >= 0) & (b < nt)
+            yield way, ok, b, target
+
+    def start_x(s):
+        for way, ok, b, target in sends(s):
+            @pl.when(ok)
+            def _():
+                x_copy(way, s, x_ref if s == 1 else x_rows(b), b, target).start()
+
+    def w_copy(which, r):
+        other = (t + r) % nt
+        source = (kw_ref, vw_ref)[which].at[
+            pl.ds(pl.multiple_of(other * chunk + p * piece, piece), piece), :
+        ]
+        return pltpu.make_async_remote_copy(
+            src_ref=source,
+            dst_ref=wide_ref.at[
+                t, pl.ds(pl.multiple_of(p * piece, piece), piece), pl.ds(which * kv, kv)
+            ],
+            send_sem=w_send.at[which, r - 1], recv_sem=w_recv.at[which, r - 1],
+            device_id={"tensor": other}, device_id_type=MESH,
+        )
+
+    def plane_copy(b, r, source):
+        q = (p + r) % plane
+        return pltpu.make_async_remote_copy(
+            src_ref=source.at[:, pl.ds(pl.multiple_of(q * slice_width, slice_width), slice_width)],
+            dst_ref=xc_ref.at[pl.ds(pl.multiple_of((p * nt + b) * rows, rows), rows), :],
+            send_sem=p_send.at[b, r - 1], recv_sem=p_recv.at[b, r - 1],
+            device_id={"dp": q // nc, "ctx": q % nc}, device_id_type=MESH,
+        )
+
+    def keep_copy(b, source):
+        return pltpu.make_async_copy(
+            source.at[:, pl.ds(pl.multiple_of(p * slice_width, slice_width), slice_width)],
+            xc_ref.at[pl.ds(pl.multiple_of((p * nt + b) * rows, rows), rows), :],
+            local_sem.at[3 + b],
+        )
+
+    def to_plane(b, source):
+        for r in range(1, plane):
+            plane_copy(b, r, source).start()
+        keep_copy(b, source).start()
+
+    def wide_at(r, q):
+        return wide_ref.at[(t + nt - r) % nt, pl.ds(pl.multiple_of(q * piece, piece), piece), :]
+
+    def fan_copy(r, j):
+        hh = (h + j) % half
+        return pltpu.make_async_remote_copy(
+            src_ref=wide_at(r, p), dst_ref=wide_at(r, p),
+            send_sem=f_send.at[r - 1, j - 1], recv_sem=f_recv.at[r - 1, j - 1],
+            device_id={"dp": (hh // nc) * 2 + core, "ctx": hh % nc}, device_id_type=MESH,
+        )
+
+    def sibling_copy(r, j):
+        hh = (h + half - j) % half
+        q = ((hh // nc) * 2 + core) * nc + hh % nc
+        return pltpu.make_async_remote_copy(
+            src_ref=wide_at(r, q), dst_ref=wide_at(r, q),
+            send_sem=s_send.at[r - 1, j], recv_sem=s_recv.at[r - 1, j],
+            device_id={"dp": d + 1 - 2 * core}, device_id_type=MESH,
+        )
+
+    start_x(1)
+    for r in range(1, nt):
+        for which in (0, 1):
+            w_copy(which, r).start()
+    own = [
+        pltpu.make_async_copy(x_ref, x_rows(t), local_sem.at[0]),
+        pltpu.make_async_copy(
+            kw_ref.at[pl.ds(pl.multiple_of(t * chunk, chunk), chunk), :],
+            wide_ref.at[t, :, pl.ds(0, kv)], local_sem.at[1],
+        ),
+        pltpu.make_async_copy(
+            vw_ref.at[pl.ds(pl.multiple_of(t * chunk, chunk), chunk), :],
+            wide_ref.at[t, :, pl.ds(kv, kv)], local_sem.at[2],
+        ),
+    ]
+    to_plane(t, x_ref)
+    for copy in own:
+        copy.start()
+    for s in range(1, nt):
+        for way in (0, 1):
+            b = t - s if way == 0 else t + s
+
+            @pl.when((b >= 0) & (b < nt))
+            def _():
+                x_copy(way, s, x_ref, b, (t + 1) % nt).wait_recv()
+
+        if s < nt - 1:
+            start_x(s + 1)
+        for way in (0, 1):
+            b = t - s if way == 0 else t + s
+
+            @pl.when((b >= 0) & (b < nt))
+            def _():
+                to_plane(b, x_rows(b))
+
+        for which in (0, 1):
+            w_copy(which, s).wait_recv()
+        for j in range(1, half):
+            fan_copy(s, j).start()
+        sibling_copy(s, 0).start()
+    for s in range(1, nt):
+        for j in range(1, half):
+            fan_copy(s, j).wait_recv()
+            sibling_copy(s, j).start()
+    for s in range(1, nt):
+        for way, ok, b, target in sends(s):
+            @pl.when(ok)
+            def _():
+                x_copy(way, s, x_ref, b, target).wait_send()
+        for which in (0, 1):
+            w_copy(which, s).wait_send()
+        for j in range(1, half):
+            fan_copy(s, j).wait_send()
+        for j in range(half):
+            sibling_copy(s, j).wait()
+    for b in range(nt):
+        for r in range(1, plane):
+            plane_copy(b, r, x_ref).wait()
+        keep_copy(b, x_ref).wait()
+    for copy in own:
+        copy.wait()
+
+
+def exchange_inputs(x, key_weight, value_weight):
+    nt, nd, nc = lax.axis_size("tensor"), lax.axis_size("dp"), lax.axis_size("ctx")
+    plane = nd * nc
+    rows, width = x.shape
+    kv = key_weight.shape[1]
+    dma = pltpu.SemaphoreType.DMA
+    return pl.pallas_call(
+        functools.partial(exchange_kernel, nt, nd, nc),
+        out_shape=(
+            jax.ShapeDtypeStruct((nt * rows, width), x.dtype),
+            jax.ShapeDtypeStruct((plane * nt * rows, width // plane), x.dtype),
+            jax.ShapeDtypeStruct((nt, width // nt, 2 * kv), x.dtype),
+        ),
+        in_specs=[pl.BlockSpec(memory_space=pltpu.HBM)] * 3,
+        out_specs=[pl.BlockSpec(memory_space=pltpu.HBM)] * 3,
+        scratch_shapes=[
+            dma((2, nt - 1)), dma((2, nt - 1)), dma((2, nt - 1)), dma((2, nt - 1)),
+            dma((nt, plane - 1)), dma((nt, plane - 1)),
+            dma((nt - 1, plane // 2 - 1)), dma((nt - 1, plane // 2 - 1)),
+            dma((nt - 1, plane // 2)), dma((nt - 1, plane // 2)),
+            dma((3 + nt,)),
+        ],
+        compiler_params=pltpu.CompilerParams(collective_id=0, has_side_effects=True),
+    )(x, key_weight, value_weight)
 
 
 def per_device(
@@ -26,21 +228,9 @@
     q_local = queries.shape[2] // HEAD_SIZE
     queries_per_group = q_local // kv_local
     kv_width = kv_local * HEAD_SIZE
-    gathered = lax.all_gather(layer_input, "tensor", axis=1, tiled=True)[0]
-    planes = lax.axis_size("tensor")
-    plane_size = lax.axis_size("dp") * lax.axis_size("ctx")
-    plane_index = lax.axis_index("dp") * lax.axis_size("ctx") + lax.axis_index("ctx")
-    model_width = key_weight.shape[0]
-    piece_rows = model_width // (planes * plane_size)
-
-    def piece(weight):
-        split = weight.reshape(planes, plane_size, piece_rows, kv_width)
-        return lax.dynamic_index_in_dim(split, plane_index, 1, keepdims=False)
-
-    pieces = jnp.concatenate([piece(key_weight), piece(value_projection_weight)], axis=2)
-    pieces = lax.all_to_all(pieces, "tensor", split_axis=0, concat_axis=0, tiled=True)
-    wide_weight = lax.all_gather(pieces, ("dp", "ctx"), axis=1, tiled=True)
-    plane_input = lax.all_to_all(gathered, ("dp", "ctx"), split_axis=1, concat_axis=0, tiled=True)
+    gathered, plane_input, wide_weight = exchange_inputs(
+        layer_input[0], key_weight, value_projection_weight
+    )
     projected_keys = jnp.dot(gathered, key_weight, preferred_element_type=jnp.float32)
     projected_values = jnp.dot(
         gathered, value_projection_weight, preferred_element_type=jnp.float32

time: 302 us -> 284 us (0.940)
  Pallas kernels: 0 us -> 116 us
  waiting for transfers between devices: 180 us -> 74.8 us
  local copies, waits for them, and re-layouts: 37.1 us -> 20.8 us
  starting transfers between devices: 16.9 us -> 4.92 us
    all_gather x2 -> x0, waiting for transfers between devices: 143 us -> none  [the longest x1 78.9 us: per_device(): wide_weight = lax.all_gather(pieces, ('dp', 'ctx'), axis=1, tiled=True)]
    pallas_call x0 -> x1, Pallas kernels: none -> 116 us  [exchange_inputs(): pl.pallas_call(functools.partial(exchange_kernel, nt, nd, nc), out_shape=...]
    all_gather x1, waiting for transfers between devices: 8.51 us -> 29 us  [per_device(): kv_all = lax.all_gather(own_grads, 'tensor', axis=0)]
    all_to_all x1, waiting for transfers between devices: 0.01 us -> 18.6 us  [per_device(): lax.all_to_all(width_part, 'tensor', split_axis=0, concat_axis=1, tiled=T...]
    reduce_scatter x1, waiting for transfers between devices: 11.7 us -> 26.4 us  [per_device(): lax.psum_scatter(keyval_sum, 'ctx', scatter_dimension=0, tiled=True)]
    all_to_all x2 -> x0, starting transfers between devices: 11.6 us -> none  [the longest x1 6.53 us: per_device(): lax.all_to_all(pieces, 'tensor', split_axis=0, concat_axis=0, tiled=True)]
    all_to_all x2 -> x0, waiting for transfers between devices: 8.2 us -> none  [the longest x1 8.19 us: per_device(): lax.all_to_all(pieces, 'tensor', split_axis=0, concat_axis=0, tiled=True)]
    all_gather x1, waiting for transfers between devices: 8.05 us -> 0.01 us  [per_device(): kv_plane = lax.all_gather(own_grads, ('dp', 'ctx'), axis=0, tiled=True)]
  transfers between devices with their start and end apart: 8 -> 4, of which waited for: 6 -> 3; matrix products, arithmetic and copies ran while one was open for 18% -> 5% of each run, Pallas kernels for 0% -> 0%
where the time goes in v2:
time: 284 us; the launch traced here: 279 us
  Pallas kernels  116 us (41%)
  waiting for transfers between devices  74.8 us (26%)
  matrix products  30.1 us (11%)
  local copies, waits for them, and re-layouts  20.8 us (7%)
  between operations  14.1 us (5%)
  other arithmetic  10 us (4%)
  blocking collectives  8.62 us (3%)
  starting transfers between devices  4.92 us (2%)
    pallas_call x1, Pallas kernels, exchange_inputs(): pl.pallas_call(functools.partial(exchange_kernel, nt, nd, nc), out_shape=...  116 us
    all_gather x1, waiting for transfers between devices, per_device(): kv_all = lax.all_gather(own_grads, 'tensor', axis=0)  29 us
    reduce_scatter x1, waiting for transfers between devices, per_device(): lax.psum_scatter(keyval_sum, 'ctx', scatter_dimension=0, tiled=True)  26.4 us
    all_to_all x1, waiting for transfers between devices, per_device(): lax.all_to_all(width_part, 'tensor', split_axis=0, concat_axis=1, tiled=T...  18.6 us
    all_gather x1, blocking collectives, per_device(): lax.all_gather(kv_rows, 'ctx', axis=0, tiled=True)  8.62 us
    dot_general x1, matrix products, per_device(): lax.dot_general(kv_all, wide_weight, (((0, 2), (0, 2)), ((), ())), prefer...  6.72 us
    unnamed x23, local copies, waits for them, and re-layouts  5.79 us
  transfers between devices with their start and end apart: 4, of which 3 were waited for; matrix products, arithmetic and copies ran while one was open for 5% of the time, Pallas kernels for 0%

profile of v2, /device:TPU:14, one launch (start us, length us, event | category | flops | bytes accessed | tf_op | source)
XLA Modules:
  0.0 279.2 jit_solution(4147751021690560968)
XLA Ops:
  7.2 0.7 bitcast_multiply_fusion
  8.0 0.7 fusion.10
  8.7 0.7 compare_and_fusion.1
  10.9 116.0 %shard_map.120 = (bf16[256,8192]{1,0:T(8,128)(2,1)}, bf16[2048,1024]{1,0:T(8,128)(2,1)}, bf16[4,2048,512]{2,1,0:T(8,128)(2,1)}) custom-call(bf16[64,8192]{1,0:T(8,128)(2,1)} %bitcast.129, bf16[8192,256]{1,0:T(8,128)(2,1)} %kw_ref.1, bf16[8192,256]{1,0:T(8,128)(2,1)} %vw_ref.1), custom_call_target="tpu_custom_call" | custom-call | tf_op jit(solution)/shard_map/pallas_call | solution.py:194
  126.9 5.3 %convolution_convert_fusion.1 = bf16[256,256]{0,1:T(8,128)(2,1)S(1)} fusion(bf16[256,8192]{1,0:T(8,128)(2,1)} %get-tuple-element.56, bf16[8192,256]{1,0:T(8,128)(2,1)} %vw_ref.1), kind=kOutput, calls=%fused_computation.22 | convolution fusion | flops 1073807360 | bytes 8519680 | tf_op jit(solution)/shard_map/dot_general | solution.py:235
  132.9 1.9 convolution_convert_fusion.2
  134.7 3.5 %gather_fusion.3 = s32[512]{0:T(512)S(1)} fusion(s32[512]{0:T(512)S(1)} %bitcast.117, s32[1024]{0:T(1024)S(1)} %pad_clamp_fusion.1), kind=kCustom, calls=%fused_computation.1.clone | custom fusion | bytes 6144 | tf_op jit(solution)/shard_map/while/body/eval_jaxpr/jit(_take)/gather | solution.py:260
  138.4 1.9 gather_fusion.1
  143.2 1.5 copy.71
  144.6 1.6 copy.53
  146.9 0.9 multiply_reduce_fusion
  148.5 8.6 %all_gather.13 = bf16[512,512]{0,1:T(8,128)(2,1)S(1)} all-gather(bf16[256,512]{0,1:T(8,128)(2,1)S(1)} %pad_maximum_fusion.1), channel_id=1, replica_groups=mesh['dp'=4,'ctx'=2,'tensor'=4] {'ctx'}, dimensions={0}, use_global_device_ids=true | all-gather | bytes 786432 | tf_op jit(solution)/shard_map/all_gather | solution.py:358
  157.2 1.4 fusion.3
  158.6 1.7 exponential_reduce_fusion
  160.3 2.3 fusion.4
  162.7 2.8 %fusion.1 = bf16[2,8,256,512]{2,3,1,0:T(8,128)(2,1)S(1)} fusion(f32[2,512,256,8]{2,1,3,0:T(8,128)S(1)} %get-tuple-element.110, f32[2,8,256]{2,1,0:T(8,128)S(1)} %copy-done.9, f32[2,8,256]{2,1,0:T(8,128)S(1)} %log_add_fusion, pred[256,512]{0,1:T(8,128)(4,1)S(1)} %copy.43, bf16[512,2,128,1]{0,2,3,1:T(8,128)(2,1)S(1)} %bitcast.135, ...), kind=kOutput, calls=%fused_computation.6 | convolution fusion | flops 549453824 | bytes 14057472 | tf_op jit(solution)/shard_map/while/body/eval_jaxpr/qhgd,khd->hgqk/dot_general | solution.py:300
  165.5 1.9 copy-done.3
  167.4 1.5 fusion.8
  168.9 1.0 pad_maximum_fusion
  170.0 26.4 %reduce-scatter.2.cloned.1.call-done = f32[256,512]{0,1:T(8,128)} async-done(((f32[512,512]{0,1:T(8,128)}), f32[256,512]{0,1:T(8,128)}) %reduce-scatter.2.cloned.1.call-update) | async-done | bytes 524304 | tf_op jit(solution)/shard_map/reduce_scatter | solution.py:360
  196.4 1.8 convert_element_type.47
  199.0 29.0 %all-gather.6.cloned.1.call-done = bf16[1024,512]{0,1:T(8,128)(2,1)} async-done(((bf16[256,512]{0,1:T(8,128)(2,1)}), bf16[1024,512]{0,1:T(8,128)(2,1)}) %all-gather.6.cloned.1.call-update) | async-done | bytes 1048592 | tf_op jit(solution)/shard_map/all_gather | solution.py:366
  228.0 1.5 copy.54
  229.5 6.7 %fusion.7 = bf16[256,2048]{1,0:T(8,128)(2,1)} fusion(bf16[4,256,512]{2,1,0:T(8,128)(2,1)S(1)} %bitcast.131, bf16[4,2048,512]{2,1,0:T(8,128)(2,1)} %get-tuple-element.57), kind=kOutput, calls=%fused_computation.15 | convolution fusion | flops 2148007936 | bytes 10485760 | tf_op jit(solution)/shard_map/dot_general | solution.py:368
  236.2 4.8 %all-to-all-start = ((bf16[4,64,2048]{2,1,0:T(8,128)(2,1)}), bf16[4,64,2048]{2,1,0:T(8,128)(2,1)S(1)}, u32[]{:S(2)}, u32[]{:S(2)}) async-start(bf16[4,64,2048]{2,1,0:T(8,128)(2,1)} %bitcast.33), calls=%async_computation.1 | async-start | bytes 2097152 | tf_op jit(solution)/shard_map/all_to_all | solution.py:371
  241.0 2.9 %multiply_convert_fusion = bf16[2,128,8,256]{3,1,2,0:T(8,128)(2,1)S(1)} fusion(bf16[512,2,128,1]{0,2,3,1:T(8,128)(2,1)S(1)} %bitcast.127, bf16[2,8,256,512]{2,3,1,0:T(8,128)(2,1)} %copy-done.3), kind=kOutput, calls=%fused_computation.17 | convolution fusion | flops 537919488 | bytes 5505024 | tf_op jit(solution)/shard_map/while/body/eval_jaxpr/hgqk,khd->qhgd/dot_general | solution.py:304
  244.0 1.4 copy.56
  245.4 18.6 %all-to-all-done = bf16[4,64,2048]{2,1,0:T(8,128)(2,1)S(1)} async-done(((bf16[4,64,2048]{2,1,0:T(8,128)(2,1)}), bf16[4,64,2048]{2,1,0:T(8,128)(2,1)S(1)}, u32[]{:S(2)}, u32[]{:S(2)}) %all-to-all-start) | async-done | bytes 1048608 | tf_op jit(solution)/shard_map/all_to_all | solution.py:371
  264.0 0.8 copy.55
  264.8 1.6 broadcast_in_dim.114
  266.4 5.3 %convolution_convert_fusion = bf16[1024,512]{1,0:T(8,128)(2,1)S(1)} fusion(bf16[2048,1024]{1,0:T(8,128)(2,1)} %get-tuple-element.72, bf16[2048,512]{0,1:T(8,128)(2,1)} %all-gather.4.cloned.1.call-done), kind=kOutput, calls=%fused_computation.19 | convolution fusion | flops 2148007936 | bytes 7340032 | tf_op jit(solution)/shard_map/dot_general | solution.py:372
  271.7 1.0 fusion.14
  (55 shorter events, 7.2 us)
Async XLA Ops:
  7.2 127.6 %copy-start = (s32[1,512]{1,0:T(1,128)S(1)}, s32[1,512]{1,0:T(1,128)}, u32[]{:S(2)}) copy-start(s32[1,512]{1,0:T(1,128)} %param.19) | copy-start | bytes 6148
  7.2 189.3 %reduce-scatter.2.cloned.1.call-start = ((), (), s32[]{:S(2)}) async-start(), calls=%async_computation.2 | async-start | bytes 1572864 | tf_op jit(solution)/shard_map/reduce_scatter | solution.py:360
  126.9 5.4 %copy-start.2 = (bf16[8192,256]{1,0:T(8,128)(2,1)S(1)}, bf16[8192,256]{1,0:T(8,128)(2,1)}, u32[]{:S(2)}) copy-start(bf16[8192,256]{1,0:T(8,128)(2,1)} %kw_ref.1) | copy-start | bytes 12582916
  126.9 5.9 %copy-start.4 = (bf16[256,8192]{1,0:T(8,128)(2,1)S(1)}, bf16[256,8192]{1,0:T(8,128)(2,1)}, u32[]{:S(2)}) copy-start(bf16[256,8192]{1,0:T(8,128)(2,1)} %get-tuple-element.56) | copy-start | bytes 12582916
  132.9 7.6 %copy-start.8 = (s32[1,4,4]{2,1,0:T(4,128)S(1)}, s32[1,4,4]{2,1,0:T(4,128)}, u32[]{:S(2)}) copy-start(s32[1,4,4]{2,1,0:T(4,128)} %param.20) | copy-start | bytes 196
  132.9 9.8 %copy-start.6 = (bf16[1,256,2048]{2,1,0:T(8,128)(2,1)S(1)}, bf16[1,256,2048]{2,1,0:T(8,128)(2,1)}, u32[]{:S(2)}) copy-start(bf16[1,256,2048]{2,1,0:T(8,128)(2,1)} %param.14) | copy-start | bytes 3145732
  138.3 8.0 %copy-start.5 = (bf16[1,256,2048]{2,1,0:T(8,128)(2,1)S(1)}, bf16[1,256,2048]{2,1,0:T(8,128)(2,1)}, u32[]{:S(2)}) copy-start(bf16[1,256,2048]{2,1,0:T(8,128)(2,1)} %param.15) | copy-start | bytes 3145732
  158.6 1.8 copy-start.7
  160.3 2.3 copy-start.9
  165.5 1.9 copy-start.3
  170.0 58.0 %all-gather.6.cloned.1.call-start = ((), (), s32[]{:S(2)}) async-start(), calls=%async_computation.4 | async-start | bytes 1310720 | tf_op jit(solution)/shard_map/all_gather | solution.py:366
  198.2 68.2 %all-gather.4.cloned.1.call-start = ((), (), s32[]{:S(2)}) async-start(), calls=%async_computation.3 | async-start | bytes 2359296 | tf_op jit(solution)/shard_map/all_gather | solution.py:367
  236.2 27.8 %all-to-all-start = ((bf16[4,64,2048]{2,1,0:T(8,128)(2,1)}), bf16[4,64,2048]{2,1,0:T(8,128)(2,1)S(1)}, u32[]{:S(2)}, u32[]{:S(2)}) async-start(bf16[4,64,2048]{2,1,0:T(8,128)(2,1)} %bitcast.33), calls=%async_computation.1 | async-start | bytes 2097152 | tf_op jit(solution)/shard_map/all_to_all | solution.py:371
  266.4 6.3 %copy-start.1 = (s32[1,512]{1,0:T(1,128)S(1)}, s32[1,512]{1,0:T(1,128)}, u32[]{:S(2)}) copy-start(s32[1,512]{1,0:T(1,128)} %param.19) | copy-start | bytes 6148
Sparse Core Ops, SparseCore 0:
  170.1 26.3 reduce-scatter.1
  198.7 29.3 all-gather.5
  230.6 27.3 all-gather.3

commit v3 on v2

--- a/solution.py
+++ b/solution.py
@@ -15,8 +15,8 @@
 
 
 def exchange_kernel(
-    nt, nd, nc, x_ref, kw_ref, vw_ref, g_ref, xc_ref, wide_ref,
-    x_send, x_recv, w_send, w_recv, p_send, p_recv, f_send, f_recv, s_send, s_recv, local_sem,
+    nt, nd, nc, x_ref, kw_ref, vw_ref, g_ref, xc4_ref, wide_ref,
+    x_send, x_recv, w_send, w_recv, p_send, p_recv, f_send, f_recv, s_send, s_recv, local_sem, x_own, w_own, keep_own,
 ):
     t = lax.axis_index("tensor")
     d = lax.axis_index("dp")
@@ -32,6 +32,9 @@
     piece = chunk // plane
     slice_width = width // plane
 
+    xc_ref = xc4_ref
+    kept_ref = xc4_ref.at[p]
+
     barrier = pltpu.get_barrier_semaphore()
     for r in range(1, nt):
         pl.semaphore_signal(
@@ -85,7 +88,7 @@
         q = (p + r) % plane
         return pltpu.make_async_remote_copy(
             src_ref=source.at[:, pl.ds(pl.multiple_of(q * slice_width, slice_width), slice_width)],
-            dst_ref=xc_ref.at[pl.ds(pl.multiple_of((p * nt + b) * rows, rows), rows), :],
+            dst_ref=xc_ref.at[p, b],
             send_sem=p_send.at[b, r - 1], recv_sem=p_recv.at[b, r - 1],
             device_id={"dp": q // nc, "ctx": q % nc}, device_id_type=MESH,
         )
@@ -93,8 +96,7 @@
     def keep_copy(b, source):
         return pltpu.make_async_copy(
             source.at[:, pl.ds(pl.multiple_of(p * slice_width, slice_width), slice_width)],
-            xc_ref.at[pl.ds(pl.multiple_of((p * nt + b) * rows, rows), rows), :],
-            local_sem.at[3 + b],
+            keep_own.at[b], local_sem.at[3 + b],
         )
 
     def to_plane(b, source):
@@ -122,50 +124,55 @@
             device_id={"dp": d + 1 - 2 * core}, device_id_type=MESH,
         )
 
-    start_x(1)
     for r in range(1, nt):
         for which in (0, 1):
             w_copy(which, r).start()
+    start_x(1)
+    own_chunk = pl.ds(pl.multiple_of(t * chunk, chunk), chunk)
+    loads = [
+        pltpu.make_async_copy(x_ref, x_own, local_sem.at[0]),
+        pltpu.make_async_copy(kw_ref.at[own_chunk, :], w_own.at[:, pl.ds(0, kv)], local_sem.at[1]),
+        pltpu.make_async_copy(vw_ref.at[own_chunk, :], w_own.at[:, pl.ds(kv, kv)], local_sem.at[2]),
+    ]
     own = [
-        pltpu.make_async_copy(x_ref, x_rows(t), local_sem.at[0]),
-        pltpu.make_async_copy(
-            kw_ref.at[pl.ds(pl.multiple_of(t * chunk, chunk), chunk), :],
-            wide_ref.at[t, :, pl.ds(0, kv)], local_sem.at[1],
-        ),
-        pltpu.make_async_copy(
-            vw_ref.at[pl.ds(pl.multiple_of(t * chunk, chunk), chunk), :],
-            wide_ref.at[t, :, pl.ds(kv, kv)], local_sem.at[2],
-        ),
+        pltpu.make_async_copy(x_own, x_rows(t), local_sem.at[0]),
+        pltpu.make_async_copy(w_own, wide_ref.at[t], local_sem.at[1]),
     ]
     to_plane(t, x_ref)
+    for copy in loads:
+        copy.start()
+    for copy in loads:
+        copy.wait()
     for copy in own:
         copy.start()
     for s in range(1, nt):
-        for way in (0, 1):
-            b = t - s if way == 0 else t + s
-
-            @pl.when((b >= 0) & (b < nt))
-            def _():
-                x_copy(way, s, x_ref, b, (t + 1) % nt).wait_recv()
-
-        if s < nt - 1:
-            start_x(s + 1)
-        for way in (0, 1):
-            b = t - s if way == 0 else t + s
-
-            @pl.when((b >= 0) & (b < nt))
-            def _():
-                to_plane(b, x_rows(b))
-
         for which in (0, 1):
             w_copy(which, s).wait_recv()
         for j in range(1, half):
             fan_copy(s, j).start()
         sibling_copy(s, 0).start()
     for s in range(1, nt):
-        for j in range(1, half):
-            fan_copy(s, j).wait_recv()
-            sibling_copy(s, j).start()
+        for way in (0, 1):
+            b = t - s if way == 0 else t + s
+
+            @pl.when((b >= 0) & (b < nt))
+            def _():
+                x_copy(way, s, x_ref, b, (t + 1) % nt).wait_recv()
+
+        if s < nt - 1:
+            start_x(s + 1)
+        for way in (0, 1):
+            b = t - s if way == 0 else t + s
+
+            @pl.when((b >= 0) & (b < nt))
+            def _():
+                to_plane(b, x_rows(b))
+
+        if s == nt - 2:
+            for r in range(1, nt):
+                for j in range(1, half):
+                    fan_copy(r, j).wait_recv()
+                    sibling_copy(r, j).start()
     for s in range(1, nt):
         for way, ok, b, target in sends(s):
             @pl.when(ok)
@@ -180,9 +187,15 @@
     for b in range(nt):
         for r in range(1, plane):
             plane_copy(b, r, x_ref).wait()
+    for b in range(nt):
         keep_copy(b, x_ref).wait()
+    keep = pltpu.make_async_copy(
+        keep_own, kept_ref, local_sem.at[2]
+    )
+    keep.start()
     for copy in own:
         copy.wait()
+    keep.wait()
 
 
 def exchange_inputs(x, key_weight, value_weight):
@@ -195,7 +208,7 @@
         functools.partial(exchange_kernel, nt, nd, nc),
         out_shape=(
             jax.ShapeDtypeStruct((nt * rows, width), x.dtype),
-            jax.ShapeDtypeStruct((plane * nt * rows, width // plane), x.dtype),
+            jax.ShapeDtypeStruct((plane, nt, rows, width // plane), x.dtype),
             jax.ShapeDtypeStruct((nt, width // nt, 2 * kv), x.dtype),
         ),
         in_specs=[pl.BlockSpec(memory_space=pltpu.HBM)] * 3,
@@ -206,9 +219,174 @@
             dma((nt - 1, plane // 2 - 1)), dma((nt - 1, plane // 2 - 1)),
             dma((nt - 1, plane // 2)), dma((nt - 1, plane // 2)),
             dma((3 + nt,)),
+            pltpu.VMEM((rows, width), x.dtype),
+            pltpu.VMEM((width // nt, 2 * kv), x.dtype),
+            pltpu.VMEM((nt, rows, width // plane), x.dtype),
         ],
         compiler_params=pltpu.CompilerParams(collective_id=0, has_side_effects=True),
     )(x, key_weight, value_weight)
+
+
+def finish_kernel(
+    nt, nd, nc, sum_ref, wide_ref, xc_ref, dx_ref, dk_ref, dv_ref,
+    part, kz, kp, wide, xc, dx_send,
+    c_send, c_recv, z_send, z_recv, p_send, p_recv, d_send, d_recv, local_sem,
+):
+    t = lax.axis_index("tensor")
+    d = lax.axis_index("dp")
+    c = lax.axis_index("ctx")
+    plane = nd * nc
+    p = d * nc + c
+    group_rows = kz.shape[1]
+    rows, chunk = dx_send.shape[1:]
+    kv = dk_ref.shape[1]
+
+    load_wide = pltpu.make_async_copy(wide_ref, wide, local_sem.at[0])
+    load_xc = pltpu.make_async_copy(xc_ref, xc, local_sem.at[1])
+    load_wide.start()
+    load_xc.start()
+    barrier = pltpu.get_barrier_semaphore()
+    for r in range(1, nt):
+        pl.semaphore_signal(
+            barrier, inc=1, device_id={"tensor": (t + r) % nt}, device_id_type=MESH
+        )
+    for r in range(1, plane):
+        q = (p + r) % plane
+        pl.semaphore_signal(
+            barrier, inc=1, device_id={"dp": q // nc, "ctx": q % nc}, device_id_type=MESH
+        )
+    pl.semaphore_wait(barrier, nt - 1 + plane - 1)
+
+    def block(i):
+        return pl.ds(pl.multiple_of(i * group_rows, group_rows), group_rows)
+
+    def part_copy(j):
+        other = (c + j) % nc
+        return pltpu.make_async_remote_copy(
+            src_ref=sum_ref.at[block(other), :], dst_ref=part.at[j - 1],
+            send_sem=c_send.at[j - 1], recv_sem=c_recv.at[j - 1],
+            device_id={"ctx": other}, device_id_type=MESH,
+        )
+
+    def z_copy(r):
+        return pltpu.make_async_remote_copy(
+            src_ref=kz.at[t], dst_ref=kz.at[t], send_sem=z_send.at[r - 1],
+            recv_sem=z_recv.at[r - 1], device_id={"tensor": (t + r) % nt}, device_id_type=MESH,
+        )
+
+    def p_copy(r):
+        q = (p + r) % plane
+        return pltpu.make_async_remote_copy(
+            src_ref=kz.at[t], dst_ref=kp.at[block(p), :], send_sem=p_send.at[r - 1],
+            recv_sem=p_recv.at[r - 1], device_id={"dp": q // nc, "ctx": q % nc},
+            device_id_type=MESH,
+        )
+
+    def dx_part(r):
+        other = (t + r) % nt
+        return pltpu.make_async_remote_copy(
+            src_ref=dx_send.at[other],
+            dst_ref=dx_ref.at[:, pl.ds(pl.multiple_of(t * chunk, chunk), chunk)],
+            send_sem=d_send.at[r - 1], recv_sem=d_recv.at[r - 1],
+            device_id={"tensor": other}, device_id_type=MESH,
+        )
+
+    for j in range(1, nc):
+        part_copy(j).start()
+    for j in range(1, nc):
+        part_copy(j).wait_recv()
+    total = sum_ref[block(c), :]
+    for j in range(1, nc):
+        total = total + part[j - 1]
+    total = total.astype(jnp.bfloat16)
+    kz[t] = total
+    kp[block(p), :] = total
+    for r in range(1, nt):
+        z_copy(r).start()
+    for r in range(1, plane):
+        p_copy(r).start()
+    load_wide.wait()
+    for r in range(1, nt):
+        z_copy(r).wait_recv()
+    tile = 256
+
+    @pl.loop(0, chunk // tile)
+    def _(n):
+        columns = pl.ds(pl.multiple_of(n * tile, tile), tile)
+        out = None
+        for b in range(nt):
+            term = lax.dot_general(
+                kz[b], wide[b, columns, :], (((1,), (1,)), ((), ())),
+                preferred_element_type=jnp.float32,
+            )
+            out = term if out is None else out + term
+        dx_send[:, :, columns] = out.astype(jnp.bfloat16).reshape(nt, rows, tile)
+
+    for r in range(1, nt):
+        dx_part(r).start()
+    keep = pltpu.make_async_copy(
+        dx_send.at[t], dx_ref.at[:, pl.ds(pl.multiple_of(t * chunk, chunk), chunk)],
+        local_sem.at[2],
+    )
+    keep.start()
+    load_xc.wait()
+    for r in range(1, plane):
+        p_copy(r).wait_recv()
+
+    @pl.loop(0, dk_ref.shape[0] // tile)
+    def _(m):
+        columns = pl.ds(pl.multiple_of(m * tile, tile), tile)
+        out = lax.dot_general(
+            xc[:, columns], kp[...], (((0,), (0,)), ((), ())),
+            preferred_element_type=jnp.float32,
+        )
+        dk_ref[columns, :] = out[:, :kv].astype(jnp.bfloat16)
+        dv_ref[columns, :] = out[:, kv:].astype(jnp.bfloat16)
+
+    for j in range(1, nc):
+        part_copy(j).wait_send()
+    for r in range(1, nt):
+        z_copy(r).wait_send()
+        dx_part(r).wait()
+    for r in range(1, plane):
+        p_copy(r).wait_send()
+    keep.wait()
+
+
+def finish_grads(keyval_sum, wide_weight, plane_input):
+    nt, nd, nc = lax.axis_size("tensor"), lax.axis_size("dp"), lax.axis_size("ctx")
+    plane = nd * nc
+    seq_rows, kv2 = keyval_sum.shape
+    group_rows = seq_rows // nc
+    chunk = wide_weight.shape[1]
+    slice_width = plane_input.shape[1]
+    low = plane_input.dtype
+    dma = pltpu.SemaphoreType.DMA
+    hbm = pl.BlockSpec(memory_space=pltpu.HBM)
+    vmem = pl.BlockSpec(memory_space=pltpu.VMEM)
+    return pl.pallas_call(
+        functools.partial(finish_kernel, nt, nd, nc),
+        out_shape=(
+            jax.ShapeDtypeStruct((group_rows // nt, chunk * nt), low),
+            jax.ShapeDtypeStruct((slice_width, kv2 // 2), low),
+            jax.ShapeDtypeStruct((slice_width, kv2 // 2), low),
+        ),
+        in_specs=[vmem, hbm, hbm],
+        out_specs=[hbm, vmem, vmem],
+        scratch_shapes=[
+            pltpu.VMEM((nc - 1, group_rows, kv2), jnp.float32),
+            pltpu.VMEM((nt, group_rows, kv2), low),
+            pltpu.VMEM((plane * group_rows, kv2), low),
+            pltpu.VMEM(wide_weight.shape, low),
+            pltpu.VMEM(plane_input.shape, low),
+            pltpu.VMEM((nt, group_rows // nt, chunk), low),
+            dma((nc - 1,)), dma((nc - 1,)), dma((nt - 1,)), dma((nt - 1,)),
+            dma((plane - 1,)), dma((plane - 1,)), dma((nt - 1,)), dma((nt - 1,)), dma((3,)),
+        ],
+        compiler_params=pltpu.CompilerParams(
+            collective_id=1, has_side_effects=True, vmem_limit_bytes=56 << 20
+        ),
+    )(keyval_sum, wide_weight, plane_input)
 
 
 def per_device(
@@ -231,6 +409,7 @@
     gathered, plane_input, wide_weight = exchange_inputs(
         layer_input[0], key_weight, value_projection_weight
     )
+    plane_input = plane_input.reshape(-1, plane_input.shape[3])
     projected_keys = jnp.dot(gathered, key_weight, preferred_element_type=jnp.float32)
     projected_values = jnp.dot(
         gathered, value_projection_weight, preferred_element_type=jnp.float32
@@ -357,23 +536,13 @@
     query_sum, keyval_sum = grads_fold(
         grads_init, lax.all_gather(kv_rows, "ctx", axis=0, tiled=True)
     )
-    own_grads = lax.psum_scatter(keyval_sum, "ctx", scatter_dimension=0, tiled=True).astype(
-        jnp.bfloat16
-    )
     query_grad = (
         (query_sum * softmax_scale).astype(jnp.bfloat16).reshape(1, local_rows, q_local * HEAD_SIZE)
     )
-    kv_all = lax.all_gather(own_grads, "tensor", axis=0)
-    kv_plane = lax.all_gather(own_grads, ("dp", "ctx"), axis=0, tiled=True)
-    width_part = lax.dot_general(
-        kv_all, wide_weight, (((0, 2), (0, 2)), ((), ())), preferred_element_type=jnp.float32
-    ).astype(jnp.bfloat16)
-    input_grad = lax.all_to_all(width_part, "tensor", split_axis=0, concat_axis=1, tiled=True)[None]
-    weight_sum = lax.dot_general(
-        plane_input, kv_plane, (((0,), (0,)), ((), ())), preferred_element_type=jnp.float32
-    )
-    key_weight_grad = weight_sum[:, :kv_width].astype(jnp.bfloat16)
-    value_weight_grad = weight_sum[:, kv_width:].astype(jnp.bfloat16)
+    input_grad, key_weight_grad, value_weight_grad = finish_grads(
+        keyval_sum, wide_weight, plane_input
+    )
+    input_grad = input_grad[None]
     return (query_grad, input_grad, key_weight_grad, value_weight_grad)
 
 

time: 284 us -> 234 us (0.82)
  waiting for transfers between devices: 74.8 us -> 0 us
  Pallas kernels: 116 us -> 177 us
  matrix products: 30.1 us -> 15.9 us
  between operations: 14.1 us -> 0.91 us
  starting transfers between devices: 4.92 us -> 0 us
    pallas_call x0 -> x1, Pallas kernels: none -> 80.1 us  [finish_grads(): pl.pallas_call(functools.partial(finish_kernel, nt, nd, nc), out_shape=(j...]
    all_gather x2 -> x0, waiting for transfers between devices: 29 us -> none  [the longest x1 29 us: per_device(): kv_all = lax.all_gather(own_grads, 'tensor', axis=0)]
    reduce_scatter x1 -> x0, waiting for transfers between devices: 26.4 us -> none  [per_device(): lax.psum_scatter(keyval_sum, 'ctx', scatter_dimension=0, tiled=True)]
    pallas_call x1, Pallas kernels: 116 us -> 96.5 us  [exchange_inputs(): pl.pallas_call(functools.partial(exchange_kernel, nt, nd, nc), out_shape=...]
    all_to_all x1 -> x0, waiting for transfers between devices: 18.6 us -> none  [per_device(): lax.all_to_all(width_part, 'tensor', split_axis=0, concat_axis=1, tiled=T...]
    dot_general x2 -> x0, matrix products: 12 us -> none  [the longest x1 6.72 us: per_device(): lax.dot_general(kv_all, wide_weight, (((0, 2), (0, 2)), ((), ())), prefer...]
    all_to_all x1 -> x0, starting transfers between devices: 4.8 us -> none  [per_device(): lax.all_to_all(width_part, 'tensor', split_axis=0, concat_axis=1, tiled=T...]
    unnamed x23 -> x18, local copies, waits for them, and re-layouts: 5.79 us -> 10.5 us
  transfers between devices with their start and end apart: 4 -> 0, of which waited for: 3 -> 0; matrix products, arithmetic and copies ran while one was open for 5% -> 0% of each run, Pallas kernels for 0% -> 0%
where the time goes in v3:
time: 234 us; the launch traced here: 230 us
  Pallas kernels  177 us (76%)
  local copies, waits for them, and re-layouts  21 us (9%)
  matrix products  15.9 us (7%)
  other arithmetic  8.32 us (4%)
  blocking collectives  7.23 us (3%)
    pallas_call x1, Pallas kernels, exchange_inputs(): pl.pallas_call(functools.partial(exchange_kernel, nt, nd, nc), out_shape=...  96.5 us
    pallas_call x1, Pallas kernels, finish_grads(): pl.pallas_call(functools.partial(finish_kernel, nt, nd, nc), out_shape=(j...  80.1 us
    unnamed x18, local copies, waits for them, and re-layouts  10.5 us
    all_gather x1, blocking collectives, per_device(): lax.all_gather(kv_rows, 'ctx', axis=0, tiled=True)  7.23 us
    dot_general x1, matrix products, per_device(): jnp.dot(gathered, value_projection_weight, preferred_element_type=jnp.flo...  5.33 us

profile of v3, /device:TPU:14, one launch (start us, length us, event | category | flops | bytes accessed | tf_op | source)
XLA Modules:
  0.0 230.1 jit_solution(2871912635006139648)
XLA Ops:
  0.7 0.7 copy-done
  1.3 0.7 bitcast_multiply_fusion
  2.0 0.7 fusion.9
  2.8 0.7 compare_and_fusion.1
  3.5 0.7 compare_and_fusion
  4.2 0.7 bitcast_multiply_fusion.1
  4.9 3.5 %gather_fusion.3 = s32[512]{0:T(512)S(1)} fusion(s32[512]{0:T(512)S(1)} %bitcast.108, s32[1024]{0:T(1024)S(1)} %pad_clamp_fusion.1), kind=kCustom, calls=%fused_computation.1.clone | custom fusion | bytes 6144 | tf_op jit(solution)/shard_map/while/body/eval_jaxpr/jit(_take)/gather | solution.py:439
  8.7 1.9 gather_fusion.1
  10.7 1.2 gather_fusion
  12.1 0.6 gather_fusion.2
  13.6 0.5 copy.71
  14.1 1.5 copy.73
  15.5 1.6 copy.54
  17.4 0.4 copy.74
  17.8 0.9 multiply_reduce_fusion
  18.8 96.5 %shard_map.120 = (bf16[256,8192]{1,0:T(8,128)(2,1)}, bf16[8,4,64,1024]{3,2,1,0:T(8,128)(2,1)}, bf16[4,2048,512]{2,1,0:T(8,128)(2,1)}) custom-call(bf16[64,8192]{1,0:T(8,128)(2,1)} %bitcast.120, bf16[8192,256]{1,0:T(8,128)(2,1)} %kw_ref.1, bf16[8192,256]{1,0:T(8,128)(2,1)} %vw_ref.1), custom_call_target="tpu_custom_call" | custom-call | tf_op jit(solution)/shard_map/pallas_call | solution.py:207
  115.3 5.3 %convolution_convert_fusion = bf16[256,256]{0,1:T(8,128)(2,1)S(1)} fusion(bf16[256,8192]{1,0:T(8,128)(2,1)} %get-tuple-element.73, bf16[8192,256]{1,0:T(8,128)(2,1)} %vw_ref.1), kind=kOutput, calls=%fused_computation.19 | convolution fusion | flops 1073807360 | bytes 8519680 | tf_op jit(solution)/shard_map/dot_general | solution.py:414
  120.7 0.6 copy-done.2
  121.2 1.9 convolution_convert_fusion.1
  123.1 7.2 %all_gather.4 = bf16[512,512]{0,1:T(8,128)(2,1)S(1)} all-gather(bf16[256,512]{0,1:T(8,128)(2,1)S(1)} %pad_maximum_fusion.1), channel_id=1, replica_groups=mesh['dp'=4,'ctx'=2,'tensor'=4] {'ctx'}, dimensions={0}, use_global_device_ids=true | all-gather | bytes 786432 | tf_op jit(solution)/shard_map/all_gather | solution.py:537
  130.4 1.4 fusion.3
  131.8 1.7 exponential_reduce_fusion
  133.6 2.3 %fusion.4 = f32[2,512,128,1]{1,2,3,0:T(8,128)S(1)} fusion(bf16[256,2,8,128]{0,3,2,1:T(8,128)(2,1)S(1)} %copy-done.5, f32[2,512,256,8]{2,1,3,0:T(8,128)S(1)} %get-tuple-element.114, f32[2,8,256]{2,1,0:T(8,128)S(1)} %log_add_fusion, pred[256,512]{0,1:T(8,128)(4,1)S(1)} %copy.43), kind=kOutput, calls=%fused_computation.12 | convolution fusion | flops 545259520 | bytes 10108928 | tf_op jit(solution)/shard_map/while/body/eval_jaxpr/hgqk,qhgd->khd/dot_general | solution.py:476
  135.9 2.9 %fusion.1 = bf16[2,8,256,512]{2,3,1,0:T(8,128)(2,1)S(1)} fusion(f32[2,512,256,8]{2,1,3,0:T(8,128)S(1)} %get-tuple-element.114, f32[2,8,256]{2,1,0:T(8,128)S(1)} %copy.48, f32[2,8,256]{2,1,0:T(8,128)S(1)} %log_add_fusion, pred[256,512]{0,1:T(8,128)(4,1)S(1)} %copy.43, bf16[512,2,128,1]{0,2,3,1:T(8,128)(2,1)S(1)} %bitcast.126, ...), kind=kOutput, calls=%fused_computation.6 | convolution fusion | flops 549453824 | bytes 14057472 | tf_op jit(solution)/shard_map/while/body/eval_jaxpr/qhgd,khd->hgqk/dot_general | solution.py:479
  138.7 1.5 fusion.7
  140.2 0.7 multiply_convert_fusion
  140.9 1.4 copy.56
  142.8 1.1 pad_maximum_fusion.sum_ref
  143.9 80.1 %shard_map.121 = (bf16[64,8192]{1,0:T(8,128)(2,1)}, bf16[1024,256]{1,0:T(8,128)(2,1)}, bf16[1024,256]{1,0:T(8,128)(2,1)}) custom-call(f32[512,512]{1,0:T(8,128)} %pad_maximum_fusion.sum_ref, bf16[4,2048,512]{2,1,0:T(8,128)(2,1)} %get-tuple-element.74.wide_ref, bf16[2048,1024]{1,0:T(8,128)(2,1)} %bitcast.115), custom_call_target="tpu_custom_call" | custom-call | tf_op jit(solution)/shard_map/pallas_call | solution.py:367
  224.1 2.3 copy.79
  226.3 1.9 copy.80
  228.2 1.9 copy.81
  (35 shorter events, 2.2 us)
Async XLA Ops:
  0.6 0.7 copy-start
  0.6 12.9 %copy-start.4 = (bf16[1,256,2048]{2,1,0:T(8,128)(2,1)S(1)}, bf16[1,256,2048]{2,1,0:T(8,128)(2,1)}, u32[]{:S(2)}) copy-start(bf16[1,256,2048]{2,1,0:T(8,128)(2,1)} %param.14) | copy-start | bytes 3145732
  8.4 8.7 %copy-start.3 = (bf16[1,256,2048]{2,1,0:T(8,128)(2,1)S(1)}, bf16[1,256,2048]{2,1,0:T(8,128)(2,1)}, u32[]{:S(2)}) copy-start(bf16[1,256,2048]{2,1,0:T(8,128)(2,1)} %param.15) | copy-start | bytes 3145732
  115.3 5.4 %copy-start.1 = (bf16[8192,256]{1,0:T(8,128)(2,1)S(1)}, bf16[8192,256]{1,0:T(8,128)(2,1)}, u32[]{:S(2)}) copy-start(bf16[8192,256]{1,0:T(8,128)(2,1)} %kw_ref.1) | copy-start | bytes 12582916
  115.3 5.9 %copy-start.2 = (bf16[256,8192]{1,0:T(8,128)(2,1)S(1)}, bf16[256,8192]{1,0:T(8,128)(2,1)}, u32[]{:S(2)}) copy-start(bf16[256,8192]{1,0:T(8,128)(2,1)} %get-tuple-element.73) | copy-start | bytes 12582916
  131.8 1.8 copy-start.5

commit v4 on v3

--- a/solution.py
+++ b/solution.py
@@ -15,8 +15,9 @@
 
 
 def exchange_kernel(
-    nt, nd, nc, x_ref, kw_ref, vw_ref, g_ref, xc4_ref, wide_ref,
-    x_send, x_recv, w_send, w_recv, p_send, p_recv, f_send, f_recv, s_send, s_recv, local_sem, x_own, w_own, keep_own,
+    nt, nd, nc, x_ref, kw_ref, vw_ref, kv_ref, xc_ref, wide_ref,
+    x_send, x_recv, w_send, w_recv, p_send, p_recv, f_send, f_recv, s_send, s_recv,
+    k_send, k_recv, local_sem, g_ref, kw, vw, sums,
 ):
     t = lax.axis_index("tensor")
     d = lax.axis_index("dp")
@@ -32,9 +33,6 @@
     piece = chunk // plane
     slice_width = width // plane
 
-    xc_ref = xc4_ref
-    kept_ref = xc4_ref.at[p]
-
     barrier = pltpu.get_barrier_semaphore()
     for r in range(1, nt):
         pl.semaphore_signal(
@@ -93,16 +91,25 @@
             device_id={"dp": q // nc, "ctx": q % nc}, device_id_type=MESH,
         )
 
-    def keep_copy(b, source):
+    def keep_copy(b):
         return pltpu.make_async_copy(
-            source.at[:, pl.ds(pl.multiple_of(p * slice_width, slice_width), slice_width)],
-            keep_own.at[b], local_sem.at[3 + b],
+            x_rows(b).at[:, pl.ds(pl.multiple_of(p * slice_width, slice_width), slice_width)],
+            xc_ref.at[p, b], local_sem.at[3 + b],
+        )
+
+    def rows_of(i):
+        return pl.ds(pl.multiple_of(i * nt * rows, nt * rows), nt * rows)
+
+    def kv_copy(j):
+        return pltpu.make_async_remote_copy(
+            src_ref=kv_ref.at[rows_of(c), :], dst_ref=kv_ref.at[rows_of(c), :],
+            send_sem=k_send.at[j - 1], recv_sem=k_recv.at[j - 1],
+            device_id={"ctx": (c + j) % nc}, device_id_type=MESH,
         )
 
     def to_plane(b, source):
         for r in range(1, plane):
             plane_copy(b, r, source).start()
-        keep_copy(b, source).start()
 
     def wide_at(r, q):
         return wide_ref.at[(t + nt - r) % nt, pl.ds(pl.multiple_of(q * piece, piece), piece), :]
@@ -128,21 +135,26 @@
         for which in (0, 1):
             w_copy(which, r).start()
     start_x(1)
-    own_chunk = pl.ds(pl.multiple_of(t * chunk, chunk), chunk)
+    to_plane(t, x_ref)
     loads = [
-        pltpu.make_async_copy(x_ref, x_own, local_sem.at[0]),
-        pltpu.make_async_copy(kw_ref.at[own_chunk, :], w_own.at[:, pl.ds(0, kv)], local_sem.at[1]),
-        pltpu.make_async_copy(vw_ref.at[own_chunk, :], w_own.at[:, pl.ds(kv, kv)], local_sem.at[2]),
+        pltpu.make_async_copy(x_ref, x_rows(t), local_sem.at[0]),
+        pltpu.make_async_copy(kw_ref, kw, local_sem.at[1]),
+        pltpu.make_async_copy(vw_ref, vw, local_sem.at[2]),
     ]
-    own = [
-        pltpu.make_async_copy(x_own, x_rows(t), local_sem.at[0]),
-        pltpu.make_async_copy(w_own, wide_ref.at[t], local_sem.at[1]),
-    ]
-    to_plane(t, x_ref)
     for copy in loads:
         copy.start()
     for copy in loads:
         copy.wait()
+    keep_copy(t).start()
+    own_chunk = pl.ds(pl.multiple_of(t * chunk, chunk), chunk)
+    own = [
+        pltpu.make_async_copy(
+            kw.at[own_chunk, :], wide_ref.at[t, :, pl.ds(0, kv)], local_sem.at[1]
+        ),
+        pltpu.make_async_copy(
+            vw.at[own_chunk, :], wide_ref.at[t, :, pl.ds(kv, kv)], local_sem.at[2]
+        ),
+    ]
     for copy in own:
         copy.start()
     for s in range(1, nt):
@@ -167,12 +179,28 @@
             @pl.when((b >= 0) & (b < nt))
             def _():
                 to_plane(b, x_rows(b))
+                keep_copy(b).start()
 
         if s == nt - 2:
             for r in range(1, nt):
                 for j in range(1, half):
                     fan_copy(r, j).wait_recv()
                     sibling_copy(r, j).start()
+    sums[...] = jnp.zeros_like(sums)
+    depth = min(1024, width)
+
+    @pl.loop(0, width // depth)
+    def _(i):
+        part = pl.ds(pl.multiple_of(i * depth, depth), depth)
+        left = g_ref[:, part]
+        sums[:, :kv] += jnp.dot(left, kw[part, :], preferred_element_type=jnp.float32)
+        sums[:, kv:] += jnp.dot(left, vw[part, :], preferred_element_type=jnp.float32)
+
+    kv_ref[rows_of(c), :] = sums[...].astype(jnp.bfloat16)
+    for j in range(1, nc):
+        kv_copy(j).start()
+    for j in range(1, nc):
+        kv_copy(j).wait()
     for s in range(1, nt):
         for way, ok, b, target in sends(s):
             @pl.when(ok)
@@ -187,15 +215,9 @@
     for b in range(nt):
         for r in range(1, plane):
             plane_copy(b, r, x_ref).wait()
-    for b in range(nt):
-        keep_copy(b, x_ref).wait()
-    keep = pltpu.make_async_copy(
-        keep_own, kept_ref, local_sem.at[2]
-    )
-    keep.start()
+        keep_copy(b).wait()
     for copy in own:
         copy.wait()
-    keep.wait()
 
 
 def exchange_inputs(x, key_weight, value_weight):
@@ -207,28 +229,35 @@
     return pl.pallas_call(
         functools.partial(exchange_kernel, nt, nd, nc),
         out_shape=(
-            jax.ShapeDtypeStruct((nt * rows, width), x.dtype),
+            jax.ShapeDtypeStruct((nc * nt * rows, 2 * kv), x.dtype),
             jax.ShapeDtypeStruct((plane, nt, rows, width // plane), x.dtype),
             jax.ShapeDtypeStruct((nt, width // nt, 2 * kv), x.dtype),
         ),
         in_specs=[pl.BlockSpec(memory_space=pltpu.HBM)] * 3,
-        out_specs=[pl.BlockSpec(memory_space=pltpu.HBM)] * 3,
+        out_specs=[
+            pl.BlockSpec(memory_space=pltpu.VMEM),
+            pl.BlockSpec(memory_space=pltpu.HBM),
+            pl.BlockSpec(memory_space=pltpu.HBM),
+        ],
         scratch_shapes=[
             dma((2, nt - 1)), dma((2, nt - 1)), dma((2, nt - 1)), dma((2, nt - 1)),
             dma((nt, plane - 1)), dma((nt, plane - 1)),
             dma((nt - 1, plane // 2 - 1)), dma((nt - 1, plane // 2 - 1)),
             dma((nt - 1, plane // 2)), dma((nt - 1, plane // 2)),
-            dma((3 + nt,)),
-            pltpu.VMEM((rows, width), x.dtype),
-            pltpu.VMEM((width // nt, 2 * kv), x.dtype),
-            pltpu.VMEM((nt, rows, width // plane), x.dtype),
+            dma((nc - 1,)), dma((nc - 1,)), dma((3 + nt,)),
+            pltpu.VMEM((nt * rows, width), x.dtype),
+            pltpu.VMEM((width, kv), x.dtype),
+            pltpu.VMEM((width, kv), x.dtype),
+            pltpu.VMEM((nt * rows, 2 * kv), jnp.float32),
         ],
-        compiler_params=pltpu.CompilerParams(collective_id=0, has_side_effects=True),
+        compiler_params=pltpu.CompilerParams(
+            collective_id=0, has_side_effects=True, vmem_limit_bytes=48 << 20
+        ),
     )(x, key_weight, value_weight)
 
 
 def finish_kernel(
-    nt, nd, nc, sum_ref, wide_ref, xc_ref, dx_ref, dk_ref, dv_ref,
+    nt, nd, nc, sum_ref, wide_ref, xc_ref, dx_ref, dw_ref,
     part, kz, kp, wide, xc, dx_send,
     c_send, c_recv, z_send, z_recv, p_send, p_recv, d_send, d_recv, local_sem,
 ):
@@ -239,7 +268,6 @@
     p = d * nc + c
     group_rows = kz.shape[1]
     rows, chunk = dx_send.shape[1:]
-    kv = dk_ref.shape[1]
 
     load_wide = pltpu.make_async_copy(wide_ref, wide, local_sem.at[0])
     load_xc = pltpu.make_async_copy(xc_ref, xc, local_sem.at[1])
@@ -333,15 +361,14 @@
     for r in range(1, plane):
         p_copy(r).wait_recv()
 
-    @pl.loop(0, dk_ref.shape[0] // tile)
+    @pl.loop(0, dw_ref.shape[0] // tile)
     def _(m):
         columns = pl.ds(pl.multiple_of(m * tile, tile), tile)
         out = lax.dot_general(
             xc[:, columns], kp[...], (((0,), (0,)), ((), ())),
             preferred_element_type=jnp.float32,
         )
-        dk_ref[columns, :] = out[:, :kv].astype(jnp.bfloat16)
-        dv_ref[columns, :] = out[:, kv:].astype(jnp.bfloat16)
+        dw_ref[columns, :] = out.astype(jnp.bfloat16)
 
     for j in range(1, nc):
         part_copy(j).wait_send()
@@ -368,11 +395,10 @@
         functools.partial(finish_kernel, nt, nd, nc),
         out_shape=(
             jax.ShapeDtypeStruct((group_rows // nt, chunk * nt), low),
-            jax.ShapeDtypeStruct((slice_width, kv2 // 2), low),
-            jax.ShapeDtypeStruct((slice_width, kv2 // 2), low),
+            jax.ShapeDtypeStruct((slice_width, kv2), low),
         ),
         in_specs=[vmem, hbm, hbm],
-        out_specs=[hbm, vmem, vmem],
+        out_specs=[hbm, vmem],
         scratch_shapes=[
             pltpu.VMEM((nc - 1, group_rows, kv2), jnp.float32),
             pltpu.VMEM((nt, group_rows, kv2), low),
@@ -406,15 +432,10 @@
     q_local = queries.shape[2] // HEAD_SIZE
     queries_per_group = q_local // kv_local
     kv_width = kv_local * HEAD_SIZE
-    gathered, plane_input, wide_weight = exchange_inputs(
+    kv_full, plane_input, wide_weight = exchange_inputs(
         layer_input[0], key_weight, value_projection_weight
     )
     plane_input = plane_input.reshape(-1, plane_input.shape[3])
-    projected_keys = jnp.dot(gathered, key_weight, preferred_element_type=jnp.float32)
-    projected_values = jnp.dot(
-        gathered, value_projection_weight, preferred_element_type=jnp.float32
-    )
-    kv_rows = jnp.concatenate([projected_keys, projected_values], axis=1).astype(jnp.bfloat16)
     owner_row = block_owner[0]
     segments_row = segment[0]
     table_row = block_table[0]
@@ -423,8 +444,16 @@
     own_blocks = lax.dynamic_slice_in_dim(owner_row, ctx_index * blocks_here, blocks_here)
     offsets = jnp.arange(BLK, dtype=jnp.int32)
     query_pos = (own_blocks[:, None] * BLK + offsets[None, :]).reshape(-1)
-    query_seg = jnp.take(segments_row, query_pos)
-    own_table = jnp.take(table_row, own_blocks, axis=0)
+    block_ids = jnp.arange(owner_row.shape[0], dtype=jnp.int32)
+    segment_blocks = segments_row.reshape(-1, BLK)
+
+    def segments_of(blocks):
+        chosen = (blocks[:, None] == block_ids[None, :])[:, :, None]
+        return jnp.sum(jnp.where(chosen, segment_blocks[None], 0), axis=1).reshape(-1)
+
+    query_seg = segments_of(own_blocks)
+    own_chosen = (own_blocks[:, None] == block_ids[None, :])[:, :, None]
+    own_table = jnp.sum(jnp.where(own_chosen, table_row[None], 0), axis=1)
     query_heads = queries[0].reshape(local_rows, kv_local, queries_per_group, HEAD_SIZE)
     grad_heads = attention_output_gradient[0].reshape(
         local_rows, kv_local, queries_per_group, HEAD_SIZE
@@ -436,8 +465,9 @@
     def allowed_for(leading_row, row_count):
         key_blocks = lax.dynamic_slice_in_dim(owner_row, leading_row // BLK, row_count // BLK)
         key_pos = (key_blocks[:, None] * BLK + offsets[None, :]).reshape(-1)
-        key_seg = jnp.take(segments_row, key_pos)
-        table_part = jnp.take(own_table, key_blocks, axis=1) == 1
+        key_seg = segments_of(key_blocks)
+        key_chosen = (key_blocks[:, None] == block_ids[None, :])[None]
+        table_part = jnp.sum(jnp.where(key_chosen, own_table[:, None, :], 0), axis=2) == 1
         table_full = jnp.broadcast_to(
             table_part[:, None, :, None], (blocks_here, BLK, row_count // BLK, BLK)
         )
@@ -522,7 +552,7 @@
         jnp.zeros((seq_rows, 2 * kv_width), jnp.float32),
     )
     running_max, running_sum = over_blocks(
-        stats_block, stats_init, lax.all_gather(kv_rows, "ctx", axis=0, tiled=True)
+        stats_block, stats_init, kv_full
     )
     log_norm = running_max + jnp.log(running_sum)
 
@@ -534,14 +564,14 @@
         )
 
     query_sum, keyval_sum = grads_fold(
-        grads_init, lax.all_gather(kv_rows, "ctx", axis=0, tiled=True)
+        grads_init, kv_full
     )
     query_grad = (
         (query_sum * softmax_scale).astype(jnp.bfloat16).reshape(1, local_rows, q_local * HEAD_SIZE)
     )
-    input_grad, key_weight_grad, value_weight_grad = finish_grads(
-        keyval_sum, wide_weight, plane_input
-    )
+    input_grad, weight_grads = finish_grads(keyval_sum, wide_weight, plane_input)
+    key_weight_grad = weight_grads[:, :kv_width]
+    value_weight_grad = weight_grads[:, kv_width:]
     input_grad = input_grad[None]
     return (query_grad, input_grad, key_weight_grad, value_weight_grad)
 

time: 234 us -> 213 us (0.910); the launches traced: 230 us -> 212 us
  matrix products: 15.9 us -> 8.58 us
  blocking collectives: 7.23 us -> 0 us
  local copies, waits for them, and re-layouts: 21 us -> 14.1 us
    gather x4 -> x0, local copies, waits for them, and re-layouts: 7.26 us -> none  [the longest x1 3.5 us: allowed_for(): key_seg = jnp.take(segments_row, key_pos)]
    all_gather x1 -> x0, blocking collectives: 7.23 us -> none  [per_device(): lax.all_gather(kv_rows, 'ctx', axis=0, tiled=True)]
    dot_general x2 -> x0, matrix products: 7.19 us -> none  [the longest x1 5.33 us: per_device(): jnp.dot(gathered, value_projection_weight, preferred_element_type=jnp.flo...]
    unnamed x18 -> x10, local copies, waits for them, and re-layouts: 10.5 us -> 7.5 us
    pallas_call x1, Pallas kernels: 80.1 us -> 83.1 us  [finish_grads(): pl.pallas_call(functools.partial(finish_kernel, nt, nd, nc), out_shape=(j...]
    reduce_sum x0 -> x4, other arithmetic: none -> 2.45 us  [the longest x2 1.54 us: segments_of(): jnp.sum(jnp.where(chosen, segment_blocks[None], 0), axis=1).reshape(-1)]
where the time goes in v4:
time: 213 us; the launch traced here: 212 us
  Pallas kernels  178 us (84%)
  local copies, waits for them, and re-layouts  14.1 us (7%)
  other arithmetic  10.3 us (5%)
  matrix products  8.58 us (4%)
    pallas_call x1, Pallas kernels, exchange_inputs(): pl.pallas_call(functools.partial(exchange_kernel, nt, nd, nc), out_shape=...  95.2 us
    pallas_call x1, Pallas kernels, finish_grads(): pl.pallas_call(functools.partial(finish_kernel, nt, nd, nc), out_shape=(j...  83.1 us
    unnamed x10, local copies, waits for them, and re-layouts  7.5 us

profile of v4, /device:TPU:14, one launch (start us, length us, event | category | flops | bytes accessed | tf_op | source)
XLA Modules:
  0.0 212.1 jit_solution(13624707161152371833)
XLA Ops:
  0.6 0.7 iota_compare_fusion
  1.4 0.7 broadcast_multiply_fusion.1
  2.0 0.7 broadcast_multiply_fusion
  2.9 0.8 select_reduce_fusion.1
  3.7 0.8 select_reduce_fusion.3
  4.4 0.1 select_reduce_fusion.2
  4.6 0.8 select_reduce_fusion
  5.4 0.1 broadcast_in_dim.231
  5.6 0.2 fusion.8
  5.8 0.3 copy.55
  6.1 1.6 copy.86
  7.7 1.5 copy.88
  9.1 1.6 copy.67
  10.7 1.5 convert_bitcast_fusion
  12.2 0.4 copy.89
  12.6 0.9 multiply_reduce_fusion
  13.6 95.2 %shard_map.120 = (bf16[512,512]{1,0:T(8,128)(2,1)S(1)}, bf16[8,4,64,1024]{3,2,1,0:T(8,128)(2,1)S(1)}, bf16[4,2048,512]{2,1,0:T(8,128)(2,1)}) custom-call(bf16[64,8192]{1,0:T(8,128)(2,1)S(1)} %bitcast.80, bf16[8192,256]{1,0:T(8,128)(2,1)} %kw_ref.1, bf16[8192,256]{1,0:T(8,128)(2,1)} %vw_ref.1), custom_call_target="tpu_custom_call" | custom-call | tf_op jit(solution)/shard_map/pallas_call | solution.py:229
  108.8 2.0 copy-done
  111.0 0.2 copy.72
  111.2 1.4 fusion.3
  112.5 1.7 exponential_reduce_fusion
  114.3 2.3 %fusion.4 = f32[2,512,128,1]{1,2,3,0:T(8,128)S(1)} fusion(bf16[256,2,8,128]{0,3,2,1:T(8,128)(2,1)S(1)} %copy-done.2, f32[2,512,256,8]{2,1,3,0:T(8,128)S(1)} %get-tuple-element.118, f32[2,8,256]{2,1,0:T(8,128)S(1)} %log_add_fusion, pred[256,512]{0,1:T(8,128)(4,1)S(1)} %copy.55), kind=kOutput, calls=%fused_computation.8 | convolution fusion | flops 545259520 | bytes 10108928 | tf_op jit(solution)/shard_map/while/body/eval_jaxpr/hgqk,qhgd->khd/dot_general | solution.py:506
  116.6 2.7 %fusion.1 = bf16[2,8,256,512]{2,3,1,0:T(8,128)(2,1)S(1)} fusion(f32[2,512,256,8]{2,1,3,0:T(8,128)S(1)} %get-tuple-element.118, f32[2,8,256]{2,1,0:T(8,128)S(1)} %copy.60, f32[2,8,256]{2,1,0:T(8,128)S(1)} %log_add_fusion, pred[256,512]{0,1:T(8,128)(4,1)S(1)} %copy.55, bf16[256,2,8,128]{0,3,2,1:T(8,128)(2,1)S(1)} %copy-done.2, ...), kind=kOutput, calls=%fused_computation.2 | convolution fusion | flops 549453824 | bytes 14057472 | tf_op jit(solution)/shard_map/while/body/eval_jaxpr/qhgd,khd->hgqk/dot_general | solution.py:509
  119.3 1.5 fusion.7
  120.8 0.7 multiply_convert_fusion
  121.5 1.4 copy.69
  123.0 0.2 copy.84
  123.2 0.2 copy.85
  123.4 1.1 pad_maximum_fusion.sum_ref
  124.5 83.1 %shard_map.121 = (bf16[64,8192]{1,0:T(8,128)(2,1)}, bf16[1024,512]{1,0:T(8,128)(2,1)}) custom-call(f32[512,512]{1,0:T(8,128)} %pad_maximum_fusion.sum_ref, bf16[4,2048,512]{2,1,0:T(8,128)(2,1)} %get-tuple-element.61.wide_ref, bf16[2048,1024]{1,0:T(8,128)(2,1)} %bitcast.79), custom_call_target="tpu_custom_call" | custom-call | tf_op jit(solution)/shard_map/pallas_call | solution.py:394
  207.6 2.2 %fusion.12 = (bf16[1024,256]{1,0:T(8,128)(2,1)}, bf16[1024,256]{1,0:T(8,128)(2,1)}) fusion(bf16[1024,512]{1,0:T(8,128)(2,1)} %get-tuple-element.79), kind=kLoop, calls=%fused_computation.36 | loop fusion | bytes 2097152 | tf_op jit(solution)/shard_map/slice | solution.py:574
  209.8 2.3 %copy.94 = bf16[1,64,8192]{2,1,0:T(8,128)(2,1)} copy(bf16[1,64,8192]{2,1,0:T(8,128)(2,1)} %bitcast.89) | data formatting | bytes 2097152
  (16 shorter events, 0.5 us)
Async XLA Ops:
  6.1 7.5 %copy-start.1 = (bf16[1,64,8192]{2,1,0:T(8,128)(2,1)S(1)}, bf16[1,64,8192]{2,1,0:T(8,128)(2,1)}, u32[]{:S(2)}) copy-start(bf16[1,64,8192]{2,1,0:T(8,128)(2,1)} %param.9) | copy-start | bytes 3145732
  108.8 2.0 copy-start
  111.1 3.1 %copy-start.2 = (bf16[256,2,8,128]{0,3,2,1:T(8,128)(2,1)S(1)}, bf16[256,2,8,128]{0,3,2,1:T(8,128)(2,1)}, u32[]{:S(2)}) copy-start(bf16[256,2,8,128]{0,3,2,1:T(8,128)(2,1)} %copy.67) | copy-start | bytes 3145732

commit v5 on v4

--- a/solution.py
+++ b/solution.py
@@ -288,25 +288,32 @@
     def block(i):
         return pl.ds(pl.multiple_of(i * group_rows, group_rows), group_rows)
 
-    def part_copy(j):
+    span = group_rows // 2
+
+    def half_block(i, e):
+        return pl.ds(pl.multiple_of(i * group_rows + e * span, span), span)
+
+    def part_copy(j, e):
         other = (c + j) % nc
         return pltpu.make_async_remote_copy(
-            src_ref=sum_ref.at[block(other), :], dst_ref=part.at[j - 1],
-            send_sem=c_send.at[j - 1], recv_sem=c_recv.at[j - 1],
+            src_ref=sum_ref.at[half_block(other, e), :],
+            dst_ref=part.at[j - 1, pl.ds(e * span, span), :],
+            send_sem=c_send.at[e, j - 1], recv_sem=c_recv.at[e, j - 1],
             device_id={"ctx": other}, device_id_type=MESH,
         )
 
-    def z_copy(r):
-        return pltpu.make_async_remote_copy(
-            src_ref=kz.at[t], dst_ref=kz.at[t], send_sem=z_send.at[r - 1],
-            recv_sem=z_recv.at[r - 1], device_id={"tensor": (t + r) % nt}, device_id_type=MESH,
-        )
-
-    def p_copy(r):
+    def z_copy(r, e):
+        own = kz.at[t, pl.ds(e * span, span), :]
+        return pltpu.make_async_remote_copy(
+            src_ref=own, dst_ref=own, send_sem=z_send.at[e, r - 1],
+            recv_sem=z_recv.at[e, r - 1], device_id={"tensor": (t + r) % nt}, device_id_type=MESH,
+        )
+
+    def p_copy(r, e):
         q = (p + r) % plane
         return pltpu.make_async_remote_copy(
-            src_ref=kz.at[t], dst_ref=kp.at[block(p), :], send_sem=p_send.at[r - 1],
-            recv_sem=p_recv.at[r - 1], device_id={"dp": q // nc, "ctx": q % nc},
+            src_ref=kz.at[t, pl.ds(e * span, span), :], dst_ref=kp.at[half_block(p, e), :],
+            send_sem=p_send.at[e, r - 1], recv_sem=p_recv.at[e, r - 1], device_id={"dp": q // nc, "ctx": q % nc},
             device_id_type=MESH,
         )
 
@@ -319,47 +326,57 @@
             device_id={"tensor": other}, device_id_type=MESH,
         )
 
-    for j in range(1, nc):
-        part_copy(j).start()
-    for j in range(1, nc):
-        part_copy(j).wait_recv()
-    total = sum_ref[block(c), :]
-    for j in range(1, nc):
-        total = total + part[j - 1]
-    total = total.astype(jnp.bfloat16)
-    kz[t] = total
-    kp[block(p), :] = total
-    for r in range(1, nt):
-        z_copy(r).start()
-    for r in range(1, plane):
-        p_copy(r).start()
+    for e in range(2):
+        for j in range(1, nc):
+            part_copy(j, e).start()
+    for e in range(2):
+        for j in range(1, nc):
+            part_copy(j, e).wait_recv()
+        total = sum_ref[half_block(c, e), :]
+        for j in range(1, nc):
+            total = total + part[j - 1, pl.ds(e * span, span), :]
+        total = total.astype(jnp.bfloat16)
+        kz[t, pl.ds(e * span, span), :] = total
+        kp[half_block(p, e), :] = total
+        for r in range(1, nt):
+            z_copy(r, e).start()
+        for r in range(1, plane):
+            p_copy(r, e).start()
     load_wide.wait()
-    for r in range(1, nt):
-        z_copy(r).wait_recv()
     tile = 256
-
-    @pl.loop(0, chunk // tile)
-    def _(n):
-        columns = pl.ds(pl.multiple_of(n * tile, tile), tile)
-        out = None
-        for b in range(nt):
-            term = lax.dot_general(
-                kz[b], wide[b, columns, :], (((1,), (1,)), ((), ())),
-                preferred_element_type=jnp.float32,
-            )
-            out = term if out is None else out + term
-        dx_send[:, :, columns] = out.astype(jnp.bfloat16).reshape(nt, rows, tile)
-
-    for r in range(1, nt):
-        dx_part(r).start()
+    targets = nt // 2
+    for e in range(2):
+        for r in range(1, nt):
+            z_copy(r, e).wait_recv()
+
+        @pl.loop(0, chunk // tile)
+        def _(n):
+            columns = pl.ds(pl.multiple_of(n * tile, tile), tile)
+            out = None
+            for b in range(nt):
+                term = lax.dot_general(
+                    kz[b, pl.ds(e * span, span), :], wide[b, columns, :],
+                    (((1,), (1,)), ((), ())), preferred_element_type=jnp.float32,
+                )
+                out = term if out is None else out + term
+            dx_send[pl.ds(e * targets, targets), :, columns] = out.astype(
+                jnp.bfloat16
+            ).reshape(targets, rows, tile)
+
+        for r in range(1, nt):
+            @pl.when(((t + r) % nt) // targets == e)
+            def _():
+                dx_part(r).start()
+
     keep = pltpu.make_async_copy(
         dx_send.at[t], dx_ref.at[:, pl.ds(pl.multiple_of(t * chunk, chunk), chunk)],
         local_sem.at[2],
     )
     keep.start()
     load_xc.wait()
-    for r in range(1, plane):
-        p_copy(r).wait_recv()
+    for e in range(2):
+        for r in range(1, plane):
+            p_copy(r, e).wait_recv()
 
     @pl.loop(0, dw_ref.shape[0] // tile)
     def _(m):
@@ -370,13 +387,15 @@
         )
         dw_ref[columns, :] = out.astype(jnp.bfloat16)
 
-    for j in range(1, nc):
-        part_copy(j).wait_send()
+    for e in range(2):
+        for j in range(1, nc):
+            part_copy(j, e).wait_send()
+        for r in range(1, nt):
+            z_copy(r, e).wait_send()
+        for r in range(1, plane):
+            p_copy(r, e).wait_send()
     for r in range(1, nt):
-        z_copy(r).wait_send()
         dx_part(r).wait()
-    for r in range(1, plane):
-        p_copy(r).wait_send()
     keep.wait()
 
 
@@ -406,8 +425,8 @@
             pltpu.VMEM(wide_weight.shape, low),
             pltpu.VMEM(plane_input.shape, low),
             pltpu.VMEM((nt, group_rows // nt, chunk), low),
-            dma((nc - 1,)), dma((nc - 1,)), dma((nt - 1,)), dma((nt - 1,)),
-            dma((plane - 1,)), dma((plane - 1,)), dma((nt - 1,)), dma((nt - 1,)), dma((3,)),
+            dma((2, nc - 1)), dma((2, nc - 1)), dma((2, nt - 1)), dma((2, nt - 1)),
+            dma((2, plane - 1)), dma((2, plane - 1)), dma((nt - 1,)), dma((nt - 1,)), dma((3,)),
         ],
         compiler_params=pltpu.CompilerParams(
             collective_id=1, has_side_effects=True, vmem_limit_bytes=56 << 20

time: 213 us -> 212 us (level); the launches traced: 212 us -> 209 us
  Pallas kernels: 178 us -> 175 us
    pallas_call x1, Pallas kernels: 83.1 us -> 79.6 us  [finish_grads(): pl.pallas_call(functools.partial(finish_kernel, nt, nd, nc), out_shape=(j...]
where the time goes in v5:
time: 212 us; the launch traced here: 209 us
  Pallas kernels  175 us (83%)
  local copies, waits for them, and re-layouts  14.1 us (7%)
  other arithmetic  10.3 us (5%)
  matrix products  8.58 us (4%)
    pallas_call x1, Pallas kernels, exchange_inputs(): pl.pallas_call(functools.partial(exchange_kernel, nt, nd, nc), out_shape=...  95.2 us
    pallas_call x1, Pallas kernels, finish_grads(): pl.pallas_call(functools.partial(finish_kernel, nt, nd, nc), out_shape=(j...  79.6 us
    unnamed x10, local copies, waits for them, and re-layouts  7.5 us

profile of v5, /device:TPU:14, one launch (start us, length us, event | category | flops | bytes accessed | tf_op | source)
XLA Modules:
  0.0 208.6 jit_solution(8738069277251683165)
XLA Ops:
  0.6 0.7 iota_compare_fusion
  1.4 0.7 broadcast_multiply_fusion.1
  2.0 0.7 broadcast_multiply_fusion
  2.9 0.8 select_reduce_fusion.1
  3.7 0.8 select_reduce_fusion.3
  4.4 0.1 select_reduce_fusion.2
  4.6 0.8 select_reduce_fusion
  5.4 0.1 broadcast_in_dim.231
  5.6 0.2 fusion.8
  5.8 0.3 copy.55
  6.1 1.6 copy.86
  7.7 1.5 copy.88
  9.1 1.6 copy.67
  10.7 1.5 convert_bitcast_fusion
  12.2 0.4 copy.89
  12.6 0.9 multiply_reduce_fusion
  13.6 95.2 %shard_map.120 = (bf16[512,512]{1,0:T(8,128)(2,1)S(1)}, bf16[8,4,64,1024]{3,2,1,0:T(8,128)(2,1)S(1)}, bf16[4,2048,512]{2,1,0:T(8,128)(2,1)}) custom-call(bf16[64,8192]{1,0:T(8,128)(2,1)S(1)} %bitcast.80, bf16[8192,256]{1,0:T(8,128)(2,1)} %kw_ref.1, bf16[8192,256]{1,0:T(8,128)(2,1)} %vw_ref.1), custom_call_target="tpu_custom_call" | custom-call | tf_op jit(solution)/shard_map/pallas_call | solution.py:229
  108.8 2.0 copy-done
  111.0 0.2 copy.72
  111.2 1.4 fusion.3
  112.5 1.7 exponential_reduce_fusion
  114.3 2.3 %fusion.4 = f32[2,512,128,1]{1,2,3,0:T(8,128)S(1)} fusion(bf16[256,2,8,128]{0,3,2,1:T(8,128)(2,1)S(1)} %copy-done.2, f32[2,512,256,8]{2,1,3,0:T(8,128)S(1)} %get-tuple-element.118, f32[2,8,256]{2,1,0:T(8,128)S(1)} %log_add_fusion, pred[256,512]{0,1:T(8,128)(4,1)S(1)} %copy.55), kind=kOutput, calls=%fused_computation.8 | convolution fusion | flops 545259520 | bytes 10108928 | tf_op jit(solution)/shard_map/while/body/eval_jaxpr/hgqk,qhgd->khd/dot_general | solution.py:525
  116.6 2.7 %fusion.1 = bf16[2,8,256,512]{2,3,1,0:T(8,128)(2,1)S(1)} fusion(f32[2,512,256,8]{2,1,3,0:T(8,128)S(1)} %get-tuple-element.118, f32[2,8,256]{2,1,0:T(8,128)S(1)} %copy.60, f32[2,8,256]{2,1,0:T(8,128)S(1)} %log_add_fusion, pred[256,512]{0,1:T(8,128)(4,1)S(1)} %copy.55, bf16[256,2,8,128]{0,3,2,1:T(8,128)(2,1)S(1)} %copy-done.2, ...), kind=kOutput, calls=%fused_computation.2 | convolution fusion | flops 549453824 | bytes 14057472 | tf_op jit(solution)/shard_map/while/body/eval_jaxpr/qhgd,khd->hgqk/dot_general | solution.py:528
  119.3 1.5 fusion.7
  120.8 0.7 multiply_convert_fusion
  121.5 1.4 copy.69
  123.0 0.2 copy.84
  123.2 0.2 copy.85
  123.4 1.1 pad_maximum_fusion.sum_ref
  124.5 79.6 %shard_map.121 = (bf16[64,8192]{1,0:T(8,128)(2,1)}, bf16[1024,512]{1,0:T(8,128)(2,1)}) custom-call(f32[512,512]{1,0:T(8,128)} %pad_maximum_fusion.sum_ref, bf16[4,2048,512]{2,1,0:T(8,128)(2,1)} %get-tuple-element.61.wide_ref, bf16[2048,1024]{1,0:T(8,128)(2,1)} %bitcast.79), custom_call_target="tpu_custom_call" | custom-call | tf_op jit(solution)/shard_map/pallas_call | solution.py:413
  204.1 2.2 %fusion.12 = (bf16[1024,256]{1,0:T(8,128)(2,1)}, bf16[1024,256]{1,0:T(8,128)(2,1)}) fusion(bf16[1024,512]{1,0:T(8,128)(2,1)} %get-tuple-element.79), kind=kLoop, calls=%fused_computation.36 | loop fusion | bytes 2097152 | tf_op jit(solution)/shard_map/slice | solution.py:593
  206.3 2.3 %copy.94 = bf16[1,64,8192]{2,1,0:T(8,128)(2,1)} copy(bf16[1,64,8192]{2,1,0:T(8,128)(2,1)} %bitcast.89) | data formatting | bytes 2097152
  (16 shorter events, 0.5 us)
Async XLA Ops:
  6.1 7.5 %copy-start.1 = (bf16[1,64,8192]{2,1,0:T(8,128)(2,1)S(1)}, bf16[1,64,8192]{2,1,0:T(8,128)(2,1)}, u32[]{:S(2)}) copy-start(bf16[1,64,8192]{2,1,0:T(8,128)(2,1)} %param.9) | copy-start | bytes 3145732
  108.8 2.0 copy-start
  111.1 3.1 %copy-start.2 = (bf16[256,2,8,128]{0,3,2,1:T(8,128)(2,1)S(1)}, bf16[256,2,8,128]{0,3,2,1:T(8,128)(2,1)}, u32[]{:S(2)}) copy-start(bf16[256,2,8,128]{0,3,2,1:T(8,128)(2,1)} %copy.67) | copy-start | bytes 3145732
